TPU v7x, 128 devices: a whole 4x4x4 slice. The times are simulated.
128 devices in a mesh: task: 4 (over y), shard: 32 (over x, z, core).
Axes of the slice: x: 4, y: 4, z: 4, core: 2. Of those that a mesh axis runs over, the one named last changes fastest.
Arguments:
- tokens: bfloat16 [4096, 4096], P(('task', 'shard')), may hold values from -600 to 600
- gain: float32 [4096], replicated, may hold values from 0.5 to 1.5
- task_ids: int32 [4096], P(('task', 'shard')), may hold values from 0 to 7, as said below
- order: int32 [4096], P(('task', 'shard')), may hold values from 0 to 31, as said below
- w_gate: bfloat16 [8, 4096, 14336], P('task', None, 'shard'), may hold values from -0.09375 to 0.09375
- w_up: bfloat16 [8, 4096, 14336], P('task', None, 'shard'), may hold values from -0.09375 to 0.09375
- w_down: bfloat16 [8, 14336, 4096], P('task', 'shard'), may hold values from -0.046875 to 0.046875
Outputs:
- mixed: bfloat16 [4096, 4096], P(('task', 'shard'))
Inputs may be any that keep to these rules, and one draw needn't show every extreme that they name: `task_ids`: in each aligned block of 32 rows (the rows of one device) at most 8 rows name any one task; one task, the same for all blocks, is named by exactly 8 rows of every block. `order`: each aligned block of 32 entries is a permutation of 0 to 31.
All inputs are finite; a program needn't handle non-finite values.
Results may differ from a plain program's by a relative error of at most 0.015.
Values may be sent and summed in bfloat16 or wider, within the bound.
No kernel may reach another device: no remote copies, remote signals or barrier semaphores. Data moves between devices by JAX's collectives and lax.ppermute only.
A program may use at most 128 MiB of HBM per device.

v0:
```python
import functools
import jax
import jax.numpy as jnp
from jax import lax
from jax.experimental import pallas as pl
from jax.experimental.pallas import tpu as pltpu
from jax.sharding import Mesh, PartitionSpec as P

CAP = 8
RING = 4
CORES = 2
EPSILON = 1e-06
F32 = jnp.float32
BF16 = jnp.bfloat16


def shift(v, axis, step):
    return lax.ppermute(v, axis, [(i, (i + step) % RING) for i in range(RING)])


def swap_cores(v):
    return lax.ppermute(v, "core", [(0, 1), (1, 0)])


CHUNK = 256
WIDE = 1024
ANYWHERE = pl.BlockSpec(memory_space=pl.ANY)
IN_VMEM = pl.BlockSpec(memory_space=pltpu.VMEM)


def in_vmem(v):
    return pltpu.with_memory_space_constraint(v, pltpu.VMEM)


def in_hbm(v):
    return pltpu.with_memory_space_constraint(v, pltpu.HBM)


def run_copies(copies):
    for copy in copies:
        copy.start()
    for copy in copies:
        copy.wait()


def pick_kernel(which_ref, wg, wu, wd, og, ou, od, sem):
    which = which_ref[0]
    run_copies(
        [
            pltpu.make_async_copy(w.at[which], o, sem.at[i])
            for i, (w, o) in enumerate(((wg, og), (wu, ou), (wd, od)))
        ]
    )


def pick(which, w_gate, w_up, w_down):
    return pl.pallas_call(
        pick_kernel,
        out_shape=[pltpu.VMEM(w.shape[1:], BF16) for w in (w_gate, w_up, w_down)],
        in_specs=[pl.BlockSpec(memory_space=pltpu.SMEM)] + [ANYWHERE] * 3,
        out_specs=[IN_VMEM] * 3,
        scratch_shapes=[pltpu.SemaphoreType.DMA((3,))],
        compiler_params=pltpu.CompilerParams(vmem_limit_bytes=1024 * 1024),
        name="pick",
    )(which, in_hbm(w_gate), in_hbm(w_up), in_hbm(w_down))


def load_kernel(core_ref, wg, wpg, wu, wpu, wd, wpd, w1, w2, sem):
    core = core_ref[0]
    part = wpd.shape[0]
    run_copies(
        [
            pltpu.make_async_copy(wg.at[core], w1.at[pl.ds(0, part)], sem.at[0]),
            pltpu.make_async_copy(wpg, w1.at[pl.ds(part, part)], sem.at[1]),
            pltpu.make_async_copy(wu.at[core], w1.at[pl.ds(2 * part, part)], sem.at[2]),
            pltpu.make_async_copy(wpu, w1.at[pl.ds(3 * part, part)], sem.at[3]),
            pltpu.make_async_copy(wd.at[core], w2.at[pl.ds(0, part)], sem.at[4]),
            pltpu.make_async_copy(wpd, w2.at[pl.ds(part, part)], sem.at[5]),
        ]
    )


def load(core, *weights):
    part, width = weights[-1].shape
    return pl.pallas_call(
        load_kernel,
        out_shape=[
            pltpu.VMEM((2 * CORES * part, width), BF16),
            pltpu.VMEM((CORES * part, width), BF16),
        ],
        in_specs=[pl.BlockSpec(memory_space=pltpu.SMEM)] + [ANYWHERE] * 6,
        out_specs=[IN_VMEM] * 2,
        scratch_shapes=[pltpu.SemaphoreType.DMA((6,))],
        compiler_params=pltpu.CompilerParams(vmem_limit_bytes=1024 * 1024),
        name="load",
    )(core, *[in_hbm(w) if w.ndim == 3 else in_vmem(w) for w in weights])


def ffn_kernel(rows, looped, *refs):
    n = len(rows)
    xs, (w1, w2), outs = refs[:n], refs[n : n + 2], refs[n + 2 : 2 * n + 2]
    x, gu, h = refs[2 * n + 2 :]
    width = w1.shape[1]
    hidden = w2.shape[0]
    starts = [sum(rows[:i]) for i in range(n)]
    for i in range(n):
        x[starts[i] : starts[i] + rows[i], :] = xs[i][...]

    def gate_and_up(at):
        gu[:, at] = lax.dot_general(
            x[...], w1[at, :], (((1,), (1,)), ((), ())), preferred_element_type=F32
        )

    if looped:

        @pl.loop(0, 2 * hidden // CHUNK)
        def _(j):
            gate_and_up(pl.ds(pl.multiple_of(j * CHUNK, CHUNK), CHUNK))

    else:
        for j in range(2 * hidden // CHUNK):
            gate_and_up(slice(j * CHUNK, (j + 1) * CHUNK))

    gate = gu[:, :hidden]
    h[...] = (gate / (1.0 + jnp.exp(-gate)) * gu[:, hidden:]).astype(BF16)

    @pl.loop(0, width // WIDE)
    def _(j):
        cols = pl.ds(pl.multiple_of(j * WIDE, WIDE), WIDE)
        y = jnp.dot(h[...], w2[:, cols], preferred_element_type=F32).astype(BF16)
        for i in range(n):
            outs[i][:, cols] = y[starts[i] : starts[i] + rows[i]]


def ffn(xs, w1, w2, looped=False):
    rows = tuple(v.shape[0] for v in xs)
    total = sum(rows)
    hidden, width = w2.shape
    n = len(xs)
    return pl.pallas_call(
        functools.partial(ffn_kernel, rows, looped),
        out_shape=[pltpu.VMEM(v.shape, BF16) for v in xs],
        in_specs=[IN_VMEM] * (n + 2),
        out_specs=[IN_VMEM] * n,
        scratch_shapes=[
            pltpu.VMEM((total, width), BF16),
            pltpu.VMEM((total, 2 * hidden), F32),
            pltpu.VMEM((total, hidden), BF16),
        ],
        compiler_params=pltpu.CompilerParams(vmem_limit_bytes=10 * 1024 * 1024),
        cost_estimate=pl.CostEstimate(
            flops=6 * total * width * hidden, transcendentals=total * hidden, bytes_accessed=0
        ),
        name="ffn",
    )(*[in_vmem(v) for v in xs], in_vmem(w1), in_vmem(w2))


def ring_gather(v, axis):
    half = v.shape[0] // 2
    plus, minus = shift(v, axis, 1), shift(v, axis, -1)
    plus2, minus2 = shift(plus[:half], axis, 1), shift(minus[half:], axis, -1)
    return jnp.concatenate([v, plus, minus, plus2, minus2], axis=0)


def add(*terms):
    total = terms[0].astype(F32)
    for term in terms[1:]:
        total = total + term.astype(F32)
    return total.astype(BF16)


def ring_scatter(v, axis):
    unit = v.shape[0] // RING
    half = unit // 2
    own, plus, minus = v[:unit], v[unit : 2 * unit], v[2 * unit : 3 * unit]
    plus2, minus2 = v[3 * unit : 3 * unit + half], v[3 * unit + half :]
    from_next, from_last = shift(plus2, axis, -1), shift(minus2, axis, 1)
    plus = jnp.concatenate([add(plus[:half], from_next), plus[half:]], axis=0)
    minus = jnp.concatenate([minus[:half], add(minus[half:], from_last)], axis=0)
    return add(own, shift(plus, axis, -1), shift(minus, axis, 1))


def first_halves(v, axis):
    half = v.shape[0] // 2
    return [shift(v[:half], axis, 1), shift(v[half:], axis, -1)]


def second_halves(v, axis):
    half = v.shape[0] // 2
    return [shift(v[half:], axis, 1), shift(v[:half], axis, -1)]


def onward(pair, axis):
    return [shift(pair[0], axis, 1), shift(pair[1], axis, -1)]


def backward(pair, axis):
    return [shift(pair[0], axis, -1), shift(pair[1], axis, 1)]


def after(*lists):
    flat = lax.optimization_barrier([v for part in lists for v in part])
    cut, out = 0, []
    for part in lists:
        out.append(flat[cut : cut + len(part)])
        cut += len(part)
    return out


def collect(own, early, late):
    half = own.shape[0] // 2
    return jnp.concatenate(
        [add(own[:half], early[1], late[0]), add(own[half:], early[0], late[1])], axis=0
    )


def layer(tokens, gain, task_ids, order, w_gate, w_up, w_down):
    local_experts = w_gate.shape[0]
    expert_count = RING * local_experts
    group = lax.axis_index("task")
    core = lax.axis_index("core")

    values = tokens.astype(F32)
    mean_square = jnp.mean(values * values, axis=-1, keepdims=True)
    normed = (values * lax.rsqrt(mean_square + EPSILON) * gain).astype(BF16)
    onehot = (task_ids[:, None] == jnp.arange(expert_count, dtype=jnp.int32)[None, :]).astype(
        jnp.int32
    )
    position = jnp.sum(jnp.cumsum(onehot, axis=0) * onehot, axis=1) - 1
    far = (task_ids // local_experts - group) % RING
    other = (task_ids + core) % CORES
    slot_index = (other * RING + far) * CAP + position
    slot_count = expert_count * CAP
    slot_range = jnp.arange(slot_count, dtype=jnp.int32)
    placing = (slot_index[:, None] == slot_range[None, :]).astype(BF16)
    outgoing = jnp.einsum("rs,rd->sd", placing, normed, preferred_element_type=F32).astype(BF16)
    per_core = slot_count // CORES
    kept, swapped = outgoing[:per_core], swap_cores(outgoing[per_core:])

    w_gate = jnp.swapaxes(w_gate, 1, 2)
    w_up = jnp.swapaxes(w_up, 1, 2)
    core_arg = core.astype(jnp.int32).reshape(1)
    swapped, which = lax.optimization_barrier((swapped, 1 - core_arg))
    sent = pick(which, w_gate, w_up, w_down)
    peers = [swap_cores(w) for w in sent]

    def for_group(k):
        at = slice(k * CAP, (k + 1) * CAP)
        return jnp.concatenate([kept[at], swapped[at]], axis=0)

    groups = [for_group(0)] + [shift(for_group(k), "task", k) for k in range(1, RING)]
    a0 = ring_gather(jnp.concatenate(groups[:2], axis=0), "x")
    b0 = ring_gather(jnp.concatenate(groups[2:], axis=0), "z")
    lead_a, lead_b = first_halves(a0, "z"), first_halves(b0, "x")
    rest_a, rest_b = second_halves(a0, "z"), second_halves(b0, "x")
    (a0, b0), peers = after([a0, b0], peers)
    w1, w2 = load(core_arg, w_gate, peers[0], w_up, peers[1], w_down, peers[2])
    (w1, w2), lead_a, lead_b = after([w1, w2], lead_a, lead_b)
    far_a, far_b = onward(lead_a, "z"), onward(lead_b, "x")
    y0 = ffn([a0, b0], w1, w2, looped=True)
    y0, rest_a, rest_b = after(y0, rest_a, rest_b)
    early = ffn(rest_a + rest_b, w1, w2)
    early, far_a, far_b = after(early, far_a, far_b)
    early_a, early_b = backward(early[:2], "z"), backward(early[2:], "x")
    far = ffn(far_a + far_b, w1, w2)
    far, lead_a, lead_b = after(far, lead_a, lead_b)
    far_a, far_b = backward(far[:2], "z"), backward(far[2:], "x")
    late = ffn(lead_a + lead_b, w1, w2)
    far_a, late_a = after(far_a, late[:2])
    far_b, late_b = after(far_b, late[2:])
    late_a = backward([add(v, w) for v, w in zip(late_a, far_a)], "z")
    late_b = backward([add(v, w) for v, w in zip(late_b, far_b)], "x")
    ya = collect(y0[0], early_a, late_a)
    yb = collect(y0[1], early_b, late_b)
    done_a = ring_scatter(ya, "x")
    done_b = ring_scatter(yb, "z")

    both = 2 * CAP
    groups = [done_a[:both], done_a[both:], done_b[:both], done_b[both:]]
    groups = [groups[0]] + [shift(groups[k], "task", -k) for k in range(1, RING)]
    kept = jnp.concatenate([v[:CAP] for v in groups], axis=0)
    swapped = swap_cores(jnp.concatenate([v[CAP:] for v in groups], axis=0))
    wanted = jnp.take(slot_index, order)
    selecting = (wanted[:, None] == slot_range[None, :]).astype(BF16)
    returned = jnp.concatenate([kept, swapped], axis=0)
    return jnp.dot(selecting, returned, preferred_element_type=F32).astype(BF16)


def solution(mesh):
    devices = mesh.devices.reshape(RING, RING, RING, CORES)
    fine = Mesh(devices, ("task", "x", "z", "core"))
    shard = ("x", "z", "core")
    every = ("task",) + shard
    placed = (
        P(every, None),
        P(),
        P(every),
        P(every),
        P("task", None, shard),
        P("task", None, shard),
        P("task", shard, None),
    )
    return jax.shard_map(
        layer, mesh=fine, in_specs=placed, out_specs=P(every, None), check_vma=False
    )
```

profile of v0, /device:TPU:0, one launch (start us, length us, event | category | flops | bytes accessed | tf_op | source)
XLA Modules:
  0.0 182.3 jit_solution(11918041565156670362)
XLA Ops:
  8.3 3.0 %collective-permute-start.6 = (bf16[16,4096]{1,0:T(8,128)(2,1)S(1)}, bf16[16,4096]{1,0:T(8,128)(2,1)S(1)}, u32[]{:S(2)}, u32[]{:S(2)}) collective-permute-start(bf16[16,4096]{1,0:T(8,128)(2,1)S(1)} %pad_maximum_fusion.8), channel_id=1, source_target_pairs={{0,64},{32,96},{64,0},{96,32},{1,65},{33,97},{65,1},{97,33},{2,66}... | collective-permute-start | bytes 393224 | tf_op jit(solution)/shard_map/ppermute | solution.py:18
  12.7 4.2 %pick.1 = (bf16[448,4096]{1,0:T(8,128)(2,1)S(1)}, bf16[448,4096]{1,0:T(8,128)(2,1)S(1)}, bf16[448,4096]{1,0:T(8,128)(2,1)S(1)}) custom-call(s32[1]{0:T(128)S(6)} %sub.23.which_ref, bf16[2,448,4096]{2,1,0:T(8,128)(2,1)} %bitcast.4, bf16[2,448,4096]{2,1,0:T(8,128)(2,1)} %bitcast.6, bf16[2,448,4096]{2,1,0:T(8,128)(2,1)} %wd.3), custom_call_target="tpu_custom_call" | custom-call | tf_op jit(solution)/shard_map/pick/pallas_call | solution.py:57
  17.6 2.8 %collective-permute-start.3 = (bf16[32,4096]{1,0:T(8,128)(2,1)S(1)}, bf16[32,4096]{1,0:T(8,128)(2,1)S(1)}, u32[]{:S(2)}, u32[]{:S(2)}) collective-permute-start(bf16[32,4096]{1,0:T(8,128)(2,1)S(1)} %pad_maximum_fusion.1), channel_id=1, source_target_pairs={{0,24},{8,0},{16,8},{24,16},{1,25},{9,1},{17,9},{25,17},{2,26},{10... | collective-permute-start | bytes 786440 | tf_op jit(solution)/shard_map/ppermute | solution.py:18
  20.6 9.5 %collective-permute-done.2 = bf16[32,4096]{1,0:T(8,128)(2,1)S(1)} collective-permute-done((bf16[32,4096]{1,0:T(8,128)(2,1)S(1)}, bf16[32,4096]{1,0:T(8,128)(2,1)S(1)}, u32[]{:S(2)}, u32[]{:S(2)}) %collective-permute-start.2) | collective-permute-done | bytes 262176 | tf_op jit(solution)/shard_map/ppermute | solution.py:18
  30.1 4.0 %collective-permute-start.9 = (bf16[32,4096]{1,0:T(8,128)(2,1)S(1)}, bf16[32,4096]{1,0:T(8,128)(2,1)S(1)}, u32[]{:S(2)}, u32[]{:S(2)}) collective-permute-start(bf16[32,4096]{1,0:T(8,128)(2,1)S(1)} %get-tuple-element.171), channel_id=1, source_target_pairs={{0,6},{2,0},{4,2},{6,4},{1,7},{3,1},{5,3},{7,5},{8,14},{10,8},{12,... | collective-permute-start | bytes 786440 | tf_op jit(solution)/shard_map/ppermute | solution.py:18
  34.4 8.3 %collective-permute-done.8 = bf16[32,4096]{1,0:T(8,128)(2,1)S(1)} collective-permute-done((bf16[32,4096]{1,0:T(8,128)(2,1)S(1)}, bf16[32,4096]{1,0:T(8,128)(2,1)S(1)}, u32[]{:S(2)}, u32[]{:S(2)}) %collective-permute-start.8) | collective-permute-done | bytes 262176 | tf_op jit(solution)/shard_map/ppermute | solution.py:18
  42.8 3.3 %collective-permute-start.5 = (bf16[16,4096]{1,0:T(8,128)(2,1)S(1)}, bf16[16,4096]{1,0:T(8,128)(2,1)S(1)}, u32[]{:S(2)}, u32[]{:S(2)}) collective-permute-start(bf16[16,4096]{1,0:T(8,128)(2,1)S(1)} %slice.206), channel_id=1, source_target_pairs={{0,24},{8,0},{16,8},{24,16},{1,25},{9,1},{17,9},{25,17},{2,26},{10... | collective-permute-start | bytes 393224 | tf_op jit(solution)/shard_map/ppermute | solution.py:18
  46.1 2.7 %collective-permute-done.4 = bf16[16,4096]{1,0:T(8,128)(2,1)S(1)} collective-permute-done((bf16[16,4096]{1,0:T(8,128)(2,1)S(1)}, bf16[16,4096]{1,0:T(8,128)(2,1)S(1)}, u32[]{:S(2)}, u32[]{:S(2)}) %collective-permute-start.4) | collective-permute-done | bytes 131104 | tf_op jit(solution)/shard_map/ppermute | solution.py:18
  48.9 3.3 %collective-permute-start.11 = (bf16[16,4096]{1,0:T(8,128)(2,1)S(1)}, bf16[16,4096]{1,0:T(8,128)(2,1)S(1)}, u32[]{:S(2)}, u32[]{:S(2)}) collective-permute-start(bf16[16,4096]{1,0:T(8,128)(2,1)S(1)} %slice.210), channel_id=1, source_target_pairs={{0,6},{2,0},{4,2},{6,4},{1,7},{3,1},{5,3},{7,5},{8,14},{10,8},{12,... | collective-permute-start | bytes 393224 | tf_op jit(solution)/shard_map/ppermute | solution.py:18
  52.2 3.2 %collective-permute-done.10 = bf16[16,4096]{1,0:T(8,128)(2,1)S(1)} collective-permute-done((bf16[16,4096]{1,0:T(8,128)(2,1)S(1)}, bf16[16,4096]{1,0:T(8,128)(2,1)S(1)}, u32[]{:S(2)}, u32[]{:S(2)}) %collective-permute-start.10) | collective-permute-done | bytes 131104 | tf_op jit(solution)/shard_map/ppermute | solution.py:18
  55.6 3.4 %collective-permute-start.16 = (bf16[64,4096]{1,0:T(8,128)(2,1)S(1)}, bf16[64,4096]{1,0:T(8,128)(2,1)S(1)}, u32[]{:S(2)}, u32[]{:S(2)}) collective-permute-start(bf16[64,4096]{1,0:T(8,128)(2,1)S(1)} %get-tuple-element.175), channel_id=1, source_target_pairs={{0,6},{2,0},{4,2},{6,4},{1,7},{3,1},{5,3},{7,5},{8,14},{10,8},{12,... | collective-permute-start | bytes 1572872 | tf_op jit(solution)/shard_map/ppermute | solution.py:18
  59.0 3.2 %collective-permute-start.18 = (bf16[64,4096]{1,0:T(8,128)(2,1)S(1)}, bf16[64,4096]{1,0:T(8,128)(2,1)S(1)}, u32[]{:S(2)}, u32[]{:S(2)}) collective-permute-start(bf16[64,4096]{1,0:T(8,128)(2,1)S(1)} %get-tuple-element.165), channel_id=1, source_target_pairs={{0,24},{8,0},{16,8},{24,16},{1,25},{9,1},{17,9},{25,17},{2,26},{10... | collective-permute-start | bytes 1572872 | tf_op jit(solution)/shard_map/ppermute | solution.py:18
  62.3 4.4 %load.1 = (bf16[1792,4096]{1,0:T(8,128)(2,1)S(1)}, bf16[896,4096]{1,0:T(8,128)(2,1)S(1)}) custom-call(s32[1]{0:T(128)} %bitcast.core_ref, bf16[2,448,4096]{2,1,0:T(8,128)(2,1)} %bitcast.5, bf16[448,4096]{1,0:T(8,128)(2,1)S(1)} %collective-permute-done.12.wpg, bf16[2,448,4096]{2,1,0:T(8,128)(2,1)} %bitcast.7, ...), custom_call_target="tpu_custom_call" | custom-call | tf_op jit(solution)/shard_map/load/pallas_call | solution.py:85
  73.7 8.5 %ffn.4 = (bf16[128,4096]{1,0:T(8,128)(2,1)S(1)}, bf16[128,4096]{1,0:T(8,128)(2,1)S(1)}) custom-call(bf16[128,4096]{1,0:T(8,128)(2,1)S(1)} %get-tuple-element.72.refs_0_, bf16[128,4096]{1,0:T(8,128)(2,1)S(1)} %get-tuple-element.73.refs_1_, bf16[1792,4096]{1,0:T(8,128)(2,1)S(1)} %get-tuple-element.79.refs_2_.refs_4_, ...), custom_call_target="tpu_custom_call" | custom-call | flops 5637144576 | tf_op jit(solution)/shard_map/ffn/pallas_call | solution.py:140
  82.3 6.5 %collective-permute-start.24 = (bf16[64,4096]{1,0:T(8,128)(2,1)S(1)}, bf16[64,4096]{1,0:T(8,128)(2,1)S(1)}, u32[]{:S(2)}, u32[]{:S(2)}) collective-permute-start(bf16[64,4096]{1,0:T(8,128)(2,1)S(1)} %collective-permute-done.16.refs_1_), channel_id=1, source_target_pairs={{0,6},{2,0},{4,2},{6,4},{1,7},{3,1},{5,3},{7,5},{8,14},{10,8},{12,... | collective-permute-start | bytes 1572872 | tf_op jit(solution)/shard_map/ppermute | solution.py:18
  88.8 3.2 %collective-permute-start.26 = (bf16[64,4096]{1,0:T(8,128)(2,1)S(1)}, bf16[64,4096]{1,0:T(8,128)(2,1)S(1)}, u32[]{:S(2)}, u32[]{:S(2)}) collective-permute-start(bf16[64,4096]{1,0:T(8,128)(2,1)S(1)} %collective-permute-done.18.refs_3_), channel_id=1, source_target_pairs={{0,24},{8,0},{16,8},{24,16},{1,25},{9,1},{17,9},{25,17},{2,26},{10... | collective-permute-start | bytes 1572872 | tf_op jit(solution)/shard_map/ppermute | solution.py:18
  92.0 6.9 %ffn.5 = (bf16[64,4096]{1,0:T(8,128)(2,1)S(1)}, bf16[64,4096]{1,0:T(8,128)(2,1)S(1)}, bf16[64,4096]{1,0:T(8,128)(2,1)S(1)}, bf16[64,4096]{1,0:T(8,128)(2,1)S(1)}) custom-call(bf16[64,4096]{1,0:T(8,128)(2,1)S(1)} %collective-permute-done.19.refs_0_, bf16[64,4096]{1,0:T(8,128)(2,1)S(1)} %collective-permute-done.20.refs_1_, ...), custom_call_target="tpu_custom_call" | custom-call | flops 5637144576 | tf_op jit(solution)/shard_map/ffn/pallas_call | solution.py:140
  100.3 6.9 %ffn.6 = (bf16[64,4096]{1,0:T(8,128)(2,1)S(1)}, bf16[64,4096]{1,0:T(8,128)(2,1)S(1)}, bf16[64,4096]{1,0:T(8,128)(2,1)S(1)}, bf16[64,4096]{1,0:T(8,128)(2,1)S(1)}) custom-call(bf16[64,4096]{1,0:T(8,128)(2,1)S(1)} %collective-permute-done.23.refs_0_, bf16[64,4096]{1,0:T(8,128)(2,1)S(1)} %collective-permute-done.24.refs_1_, ...), custom_call_target="tpu_custom_call" | custom-call | flops 5637144576 | tf_op jit(solution)/shard_map/ffn/pallas_call | solution.py:140
  107.2 3.8 %collective-permute-start.39 = (bf16[64,4096]{1,0:T(8,128)(2,1)S(1)}, bf16[64,4096]{1,0:T(8,128)(2,1)S(1)}, u32[]{:S(2)}, u32[]{:S(2)}) collective-permute-start(bf16[64,4096]{1,0:T(8,128)(2,1)S(1)} %get-tuple-element.120), channel_id=1, source_target_pairs={{0,24},{8,0},{16,8},{24,16},{1,25},{9,1},{17,9},{25,17},{2,26},{10... | collective-permute-start | bytes 1572872 | tf_op jit(solution)/shard_map/ppermute | solution.py:18
  116.1 6.9 %ffn.7 = (bf16[64,4096]{1,0:T(8,128)(2,1)S(1)}, bf16[64,4096]{1,0:T(8,128)(2,1)S(1)}, bf16[64,4096]{1,0:T(8,128)(2,1)S(1)}, bf16[64,4096]{1,0:T(8,128)(2,1)S(1)}) custom-call(bf16[64,4096]{1,0:T(8,128)(2,1)S(1)} %collective-permute-done.15.refs_0_, bf16[64,4096]{1,0:T(8,128)(2,1)S(1)} %collective-permute-done.16.refs_1_, ...), custom_call_target="tpu_custom_call" | custom-call | flops 5637144576 | tf_op jit(solution)/shard_map/ffn/pallas_call | solution.py:140
  123.3 3.1 %collective-permute-start.31 = (bf16[64,4096]{1,0:T(8,128)(2,1)S(1)}, bf16[64,4096]{1,0:T(8,128)(2,1)S(1)}, u32[]{:S(2)}, u32[]{:S(2)}) collective-permute-start(bf16[64,4096]{1,0:T(8,128)(2,1)S(1)} %get-tuple-element.115), channel_id=1, source_target_pairs={{0,6},{2,0},{4,2},{6,4},{1,7},{3,1},{5,3},{7,5},{8,14},{10,8},{12,... | collective-permute-start | bytes 1572872 | tf_op jit(solution)/shard_map/ppermute | solution.py:18
  126.6 8.6 %collective-permute-done.29 = bf16[64,4096]{1,0:T(8,128)(2,1)S(1)} collective-permute-done((bf16[64,4096]{1,0:T(8,128)(2,1)S(1)}, bf16[64,4096]{1,0:T(8,128)(2,1)S(1)}, u32[]{:S(2)}, u32[]{:S(2)}) %collective-permute-start.29) | collective-permute-done | bytes 524320 | tf_op jit(solution)/shard_map/ppermute | solution.py:18
  135.2 2.7 %collective-permute-start.41 = (bf16[64,4096]{1,0:T(8,128)(2,1)S(1)}, bf16[64,4096]{1,0:T(8,128)(2,1)S(1)}, u32[]{:S(2)}, u32[]{:S(2)}) collective-permute-start(bf16[64,4096]{1,0:T(8,128)(2,1)S(1)} %add_convert_fusion.3), channel_id=1, source_target_pairs={{0,24},{8,0},{16,8},{24,16},{1,25},{9,1},{17,9},{25,17},{2,26},{10... | collective-permute-start | bytes 1572872 | tf_op jit(solution)/shard_map/ppermute | solution.py:18
  138.5 3.2 %collective-permute-start.30 = (bf16[64,4096]{1,0:T(8,128)(2,1)S(1)}, bf16[64,4096]{1,0:T(8,128)(2,1)S(1)}, u32[]{:S(2)}, u32[]{:S(2)}) collective-permute-start(bf16[64,4096]{1,0:T(8,128)(2,1)S(1)} %add_convert_fusion.7), channel_id=1, source_target_pairs={{0,6},{2,0},{4,2},{6,4},{1,7},{3,1},{5,3},{7,5},{8,14},{10,8},{12,... | collective-permute-start | bytes 1572872 | tf_op jit(solution)/shard_map/ppermute | solution.py:18
  142.2 3.7 %collective-permute-done.41 = bf16[64,4096]{1,0:T(8,128)(2,1)S(1)} collective-permute-done((bf16[64,4096]{1,0:T(8,128)(2,1)S(1)}, bf16[64,4096]{1,0:T(8,128)(2,1)S(1)}, u32[]{:S(2)}, u32[]{:S(2)}) %collective-permute-start.41) | collective-permute-done | bytes 524320 | tf_op jit(solution)/shard_map/ppermute | solution.py:18
  146.0 4.0 %collective-permute-done.43 = bf16[64,4096]{1,0:T(8,128)(2,1)S(1)} collective-permute-done((bf16[64,4096]{1,0:T(8,128)(2,1)S(1)}, bf16[64,4096]{1,0:T(8,128)(2,1)S(1)}, u32[]{:S(2)}, u32[]{:S(2)}) %collective-permute-start.43) | collective-permute-done | bytes 524320 | tf_op jit(solution)/shard_map/ppermute | solution.py:18
  152.9 3.3 %collective-permute-start.44 = (bf16[16,4096]{1,0:T(8,128)(2,1)S(1)}, bf16[16,4096]{1,0:T(8,128)(2,1)S(1)}, u32[]{:S(2)}, u32[]{:S(2)}) collective-permute-start(bf16[16,4096]{1,0:T(8,128)(2,1)S(1)} %get-tuple-element.133), channel_id=1, source_target_pairs={{0,6},{2,0},{4,2},{6,4},{1,7},{3,1},{5,3},{7,5},{8,14},{10,8},{12,... | collective-permute-start | bytes 393224 | tf_op jit(solution)/shard_map/ppermute | solution.py:18
  156.3 3.3 %collective-permute-start.33 = (bf16[16,4096]{1,0:T(8,128)(2,1)S(1)}, bf16[16,4096]{1,0:T(8,128)(2,1)S(1)}, u32[]{:S(2)}, u32[]{:S(2)}) collective-permute-start(bf16[16,4096]{1,0:T(8,128)(2,1)S(1)} %get-tuple-element.136), channel_id=1, source_target_pairs={{0,24},{8,0},{16,8},{24,16},{1,25},{9,1},{17,9},{25,17},{2,26},{10... | collective-permute-start | bytes 393224 | tf_op jit(solution)/shard_map/ppermute | solution.py:18
  159.8 3.3 %collective-permute-start.45 = (bf16[32,4096]{1,0:T(8,128)(2,1)S(1)}, bf16[32,4096]{1,0:T(8,128)(2,1)S(1)}, u32[]{:S(2)}, u32[]{:S(2)}) collective-permute-start(bf16[32,4096]{1,0:T(8,128)(2,1)S(1)} %pad_maximum_fusion.4), channel_id=1, source_target_pairs={{0,6},{2,0},{4,2},{6,4},{1,7},{3,1},{5,3},{7,5},{8,14},{10,8},{12,... | collective-permute-start | bytes 786440 | tf_op jit(solution)/shard_map/ppermute | solution.py:18
  163.3 3.3 %collective-permute-start.34 = (bf16[32,4096]{1,0:T(8,128)(2,1)S(1)}, bf16[32,4096]{1,0:T(8,128)(2,1)S(1)}, u32[]{:S(2)}, u32[]{:S(2)}) collective-permute-start(bf16[32,4096]{1,0:T(8,128)(2,1)S(1)} %pad_maximum_fusion.2), channel_id=1, source_target_pairs={{0,24},{8,0},{16,8},{24,16},{1,25},{9,1},{17,9},{25,17},{2,26},{10... | collective-permute-start | bytes 786440 | tf_op jit(solution)/shard_map/ppermute | solution.py:18
  167.4 3.4 %collective-permute-done.36 = bf16[32,4096]{1,0:T(8,128)(2,1)S(1)} collective-permute-done((bf16[32,4096]{1,0:T(8,128)(2,1)S(1)}, bf16[32,4096]{1,0:T(8,128)(2,1)S(1)}, u32[]{:S(2)}, u32[]{:S(2)}) %collective-permute-start.36) | collective-permute-done | bytes 262176 | tf_op jit(solution)/shard_map/ppermute | solution.py:18
  176.0 3.6 %collective-permute-done.48 = bf16[16,4096]{1,0:T(8,128)(2,1)S(1)} collective-permute-done((bf16[16,4096]{1,0:T(8,128)(2,1)S(1)}, bf16[16,4096]{1,0:T(8,128)(2,1)S(1)}, u32[]{:S(2)}, u32[]{:S(2)}) %collective-permute-start.48) | collective-permute-done | bytes 131104 | tf_op jit(solution)/shard_map/ppermute | solution.py:18
  (140 shorter events, 38.0 us)
Async XLA Ops:
  6.5 11.0 %collective-permute-start.1 = (bf16[16,4096]{1,0:T(8,128)(2,1)S(1)}, bf16[16,4096]{1,0:T(8,128)(2,1)S(1)}, u32[]{:S(2)}, u32[]{:S(2)}) collective-permute-start(bf16[16,4096]{1,0:T(8,128)(2,1)S(1)} %pad_maximum_fusion.7), channel_id=1, source_target_pairs={{0,32},{32,64},{64,96},{96,0},{1,33},{33,65},{65,97},{97,1},{2,34}... | collective-permute-start | bytes 393224 | tf_op jit(solution)/shard_map/ppermute | solution.py:18
  8.3 9.4 %collective-permute-start.6 = (bf16[16,4096]{1,0:T(8,128)(2,1)S(1)}, bf16[16,4096]{1,0:T(8,128)(2,1)S(1)}, u32[]{:S(2)}, u32[]{:S(2)}) collective-permute-start(bf16[16,4096]{1,0:T(8,128)(2,1)S(1)} %pad_maximum_fusion.8), channel_id=1, source_target_pairs={{0,64},{32,96},{64,0},{96,32},{1,65},{33,97},{65,1},{97,33},{2,66}... | collective-permute-start | bytes 393224 | tf_op jit(solution)/shard_map/ppermute | solution.py:18
  16.9 38.6 %collective-permute-start.12 = (bf16[448,4096]{1,0:T(8,128)(2,1)S(1)}, bf16[448,4096]{1,0:T(8,128)(2,1)S(1)}, u32[]{:S(2)}, u32[]{:S(2)}) collective-permute-start(bf16[448,4096]{1,0:T(8,128)(2,1)S(1)} %get-tuple-element.69), channel_id=1, source_target_pairs={{0,1},{1,0},{2,3},{3,2},{4,5},{5,4},{6,7},{7,6},{8,9},{9,8},{10,11... | collective-permute-start | bytes 11010056 | tf_op jit(solution)/shard_map/ppermute | solution.py:22
  17.0 42.0 %collective-permute-start.13 = (bf16[448,4096]{1,0:T(8,128)(2,1)S(1)}, bf16[448,4096]{1,0:T(8,128)(2,1)S(1)}, u32[]{:S(2)}, u32[]{:S(2)}) collective-permute-start(bf16[448,4096]{1,0:T(8,128)(2,1)S(1)} %get-tuple-element.70), channel_id=1, source_target_pairs={{0,1},{1,0},{2,3},{3,2},{4,5},{5,4},{6,7},{7,6},{8,9},{9,8},{10,11... | collective-permute-start | bytes 11010056 | tf_op jit(solution)/shard_map/ppermute | solution.py:22
  17.5 44.7 %collective-permute-start.14 = (bf16[448,4096]{1,0:T(8,128)(2,1)S(1)}, bf16[448,4096]{1,0:T(8,128)(2,1)S(1)}, u32[]{:S(2)}, u32[]{:S(2)}) collective-permute-start(bf16[448,4096]{1,0:T(8,128)(2,1)S(1)} %get-tuple-element.71), channel_id=1, source_target_pairs={{0,1},{1,0},{2,3},{3,2},{4,5},{5,4},{6,7},{7,6},{8,9},{9,8},{10,11... | collective-permute-start | bytes 11010056 | tf_op jit(solution)/shard_map/ppermute | solution.py:22
  17.6 16.6 %collective-permute-start.3 = (bf16[32,4096]{1,0:T(8,128)(2,1)S(1)}, bf16[32,4096]{1,0:T(8,128)(2,1)S(1)}, u32[]{:S(2)}, u32[]{:S(2)}) collective-permute-start(bf16[32,4096]{1,0:T(8,128)(2,1)S(1)} %pad_maximum_fusion.1), channel_id=1, source_target_pairs={{0,24},{8,0},{16,8},{24,16},{1,25},{9,1},{17,9},{25,17},{2,26},{10... | collective-permute-start | bytes 786440 | tf_op jit(solution)/shard_map/ppermute | solution.py:18
  20.5 9.6 %collective-permute-start.2 = (bf16[32,4096]{1,0:T(8,128)(2,1)S(1)}, bf16[32,4096]{1,0:T(8,128)(2,1)S(1)}, u32[]{:S(2)}, u32[]{:S(2)}) collective-permute-start(bf16[32,4096]{1,0:T(8,128)(2,1)S(1)} %pad_maximum_fusion.1), channel_id=1, source_target_pairs={{0,8},{8,16},{16,24},{24,0},{1,9},{9,17},{17,25},{25,1},{2,10},{10... | collective-permute-start | bytes 786440 | tf_op jit(solution)/shard_map/ppermute | solution.py:18
  30.1 12.6 %collective-permute-start.9 = (bf16[32,4096]{1,0:T(8,128)(2,1)S(1)}, bf16[32,4096]{1,0:T(8,128)(2,1)S(1)}, u32[]{:S(2)}, u32[]{:S(2)}) collective-permute-start(bf16[32,4096]{1,0:T(8,128)(2,1)S(1)} %get-tuple-element.171), channel_id=1, source_target_pairs={{0,6},{2,0},{4,2},{6,4},{1,7},{3,1},{5,3},{7,5},{8,14},{10,8},{12,... | collective-permute-start | bytes 786440 | tf_op jit(solution)/shard_map/ppermute | solution.py:18
  55.4 12.0 %collective-permute-start.15 = (bf16[64,4096]{1,0:T(8,128)(2,1)S(1)}, bf16[64,4096]{1,0:T(8,128)(2,1)S(1)}, u32[]{:S(2)}, u32[]{:S(2)}) collective-permute-start(bf16[64,4096]{1,0:T(8,128)(2,1)S(1)} %pad_maximum_fusion), channel_id=1, source_target_pairs={{0,2},{2,4},{4,6},{6,0},{1,3},{3,5},{5,7},{7,1},{8,10},{10,12},{12... | collective-permute-start | bytes 1572872 | tf_op jit(solution)/shard_map/ppermute | solution.py:18
  55.4 11.9 %collective-permute-start.17 = (bf16[64,4096]{1,0:T(8,128)(2,1)S(1)}, bf16[64,4096]{1,0:T(8,128)(2,1)S(1)}, u32[]{:S(2)}, u32[]{:S(2)}) collective-permute-start(bf16[64,4096]{1,0:T(8,128)(2,1)S(1)} %get-tuple-element.150), channel_id=1, source_target_pairs={{0,8},{8,16},{16,24},{24,0},{1,9},{9,17},{17,25},{25,1},{2,10},{10... | collective-permute-start | bytes 1572872 | tf_op jit(solution)/shard_map/ppermute | solution.py:18
  55.6 15.8 %collective-permute-start.16 = (bf16[64,4096]{1,0:T(8,128)(2,1)S(1)}, bf16[64,4096]{1,0:T(8,128)(2,1)S(1)}, u32[]{:S(2)}, u32[]{:S(2)}) collective-permute-start(bf16[64,4096]{1,0:T(8,128)(2,1)S(1)} %get-tuple-element.175), channel_id=1, source_target_pairs={{0,6},{2,0},{4,2},{6,4},{1,7},{3,1},{5,3},{7,5},{8,14},{10,8},{12,... | collective-permute-start | bytes 1572872 | tf_op jit(solution)/shard_map/ppermute | solution.py:18
  59.0 14.7 %collective-permute-start.18 = (bf16[64,4096]{1,0:T(8,128)(2,1)S(1)}, bf16[64,4096]{1,0:T(8,128)(2,1)S(1)}, u32[]{:S(2)}, u32[]{:S(2)}) collective-permute-start(bf16[64,4096]{1,0:T(8,128)(2,1)S(1)} %get-tuple-element.165), channel_id=1, source_target_pairs={{0,24},{8,0},{16,8},{24,16},{1,25},{9,1},{17,9},{25,17},{2,26},{10... | collective-permute-start | bytes 1572872 | tf_op jit(solution)/shard_map/ppermute | solution.py:18
  62.2 19.9 %collective-permute-start.20 = (bf16[64,4096]{1,0:T(8,128)(2,1)S(1)}, bf16[64,4096]{1,0:T(8,128)(2,1)S(1)}, u32[]{:S(2)}, u32[]{:S(2)}) collective-permute-start(bf16[64,4096]{1,0:T(8,128)(2,1)S(1)} %pad_maximum_fusion), channel_id=1, source_target_pairs={{0,6},{2,0},{4,2},{6,4},{1,7},{3,1},{5,3},{7,5},{8,14},{10,8},{12,... | collective-permute-start | bytes 1572872 | tf_op jit(solution)/shard_map/ppermute | solution.py:18
  67.4 14.8 %collective-permute-start.22 = (bf16[64,4096]{1,0:T(8,128)(2,1)S(1)}, bf16[64,4096]{1,0:T(8,128)(2,1)S(1)}, u32[]{:S(2)}, u32[]{:S(2)}) collective-permute-start(bf16[64,4096]{1,0:T(8,128)(2,1)S(1)} %get-tuple-element.150), channel_id=1, source_target_pairs={{0,24},{8,0},{16,8},{24,16},{1,25},{9,1},{17,9},{25,17},{2,26},{10... | collective-permute-start | bytes 1572872 | tf_op jit(solution)/shard_map/ppermute | solution.py:18
  67.4 14.8 %collective-permute-start.19 = (bf16[64,4096]{1,0:T(8,128)(2,1)S(1)}, bf16[64,4096]{1,0:T(8,128)(2,1)S(1)}, u32[]{:S(2)}, u32[]{:S(2)}) collective-permute-start(bf16[64,4096]{1,0:T(8,128)(2,1)S(1)} %get-tuple-element.175), channel_id=1, source_target_pairs={{0,2},{2,4},{4,6},{6,0},{1,3},{3,5},{5,7},{7,1},{8,10},{10,12},{12... | collective-permute-start | bytes 1572872 | tf_op jit(solution)/shard_map/ppermute | solution.py:18
  71.3 10.9 %collective-permute-start.21 = (bf16[64,4096]{1,0:T(8,128)(2,1)S(1)}, bf16[64,4096]{1,0:T(8,128)(2,1)S(1)}, u32[]{:S(2)}, u32[]{:S(2)}) collective-permute-start(bf16[64,4096]{1,0:T(8,128)(2,1)S(1)} %get-tuple-element.165), channel_id=1, source_target_pairs={{0,8},{8,16},{16,24},{24,0},{1,9},{9,17},{17,25},{25,1},{2,10},{10... | collective-permute-start | bytes 1572872 | tf_op jit(solution)/shard_map/ppermute | solution.py:18
  82.2 16.7 %collective-permute-start.23 = (bf16[64,4096]{1,0:T(8,128)(2,1)S(1)}, bf16[64,4096]{1,0:T(8,128)(2,1)S(1)}, u32[]{:S(2)}, u32[]{:S(2)}) collective-permute-start(bf16[64,4096]{1,0:T(8,128)(2,1)S(1)} %collective-permute-done.15.refs_0_), channel_id=1, source_target_pairs={{0,2},{2,4},{4,6},{6,0},{1,3},{3,5},{5,7},{7,1},{8,10},{10,12},{12... | collective-permute-start | bytes 1572872 | tf_op jit(solution)/shard_map/ppermute | solution.py:18
  82.3 16.6 %collective-permute-start.24 = (bf16[64,4096]{1,0:T(8,128)(2,1)S(1)}, bf16[64,4096]{1,0:T(8,128)(2,1)S(1)}, u32[]{:S(2)}, u32[]{:S(2)}) collective-permute-start(bf16[64,4096]{1,0:T(8,128)(2,1)S(1)} %collective-permute-done.16.refs_1_), channel_id=1, source_target_pairs={{0,6},{2,0},{4,2},{6,4},{1,7},{3,1},{5,3},{7,5},{8,14},{10,8},{12,... | collective-permute-start | bytes 1572872 | tf_op jit(solution)/shard_map/ppermute | solution.py:18
  88.8 10.4 %collective-permute-start.25 = (bf16[64,4096]{1,0:T(8,128)(2,1)S(1)}, bf16[64,4096]{1,0:T(8,128)(2,1)S(1)}, u32[]{:S(2)}, u32[]{:S(2)}) collective-permute-start(bf16[64,4096]{1,0:T(8,128)(2,1)S(1)} %collective-permute-done.17.refs_2_), channel_id=1, source_target_pairs={{0,8},{8,16},{16,24},{24,0},{1,9},{9,17},{17,25},{25,1},{2,10},{10... | collective-permute-start | bytes 1572872 | tf_op jit(solution)/shard_map/ppermute | solution.py:18
  88.8 11.5 %collective-permute-start.26 = (bf16[64,4096]{1,0:T(8,128)(2,1)S(1)}, bf16[64,4096]{1,0:T(8,128)(2,1)S(1)}, u32[]{:S(2)}, u32[]{:S(2)}) collective-permute-start(bf16[64,4096]{1,0:T(8,128)(2,1)S(1)} %collective-permute-done.18.refs_3_), channel_id=1, source_target_pairs={{0,24},{8,0},{16,8},{24,16},{1,25},{9,1},{17,9},{25,17},{2,26},{10... | collective-permute-start | bytes 1572872 | tf_op jit(solution)/shard_map/ppermute | solution.py:18
  107.2 15.8 %collective-permute-start.39 = (bf16[64,4096]{1,0:T(8,128)(2,1)S(1)}, bf16[64,4096]{1,0:T(8,128)(2,1)S(1)}, u32[]{:S(2)}, u32[]{:S(2)}) collective-permute-start(bf16[64,4096]{1,0:T(8,128)(2,1)S(1)} %get-tuple-element.120), channel_id=1, source_target_pairs={{0,24},{8,0},{16,8},{24,16},{1,25},{9,1},{17,9},{25,17},{2,26},{10... | collective-permute-start | bytes 1572872 | tf_op jit(solution)/shard_map/ppermute | solution.py:18
  111.0 12.3 %collective-permute-start.40 = (bf16[64,4096]{1,0:T(8,128)(2,1)S(1)}, bf16[64,4096]{1,0:T(8,128)(2,1)S(1)}, u32[]{:S(2)}, u32[]{:S(2)}) collective-permute-start(bf16[64,4096]{1,0:T(8,128)(2,1)S(1)} %get-tuple-element.121), channel_id=1, source_target_pairs={{0,8},{8,16},{16,24},{24,0},{1,9},{9,17},{17,25},{25,1},{2,10},{10... | collective-permute-start | bytes 1572872 | tf_op jit(solution)/shard_map/ppermute | solution.py:18
  111.0 27.3 %collective-permute-start.38 = (bf16[64,4096]{1,0:T(8,128)(2,1)S(1)}, bf16[64,4096]{1,0:T(8,128)(2,1)S(1)}, u32[]{:S(2)}, u32[]{:S(2)}) collective-permute-start(bf16[64,4096]{1,0:T(8,128)(2,1)S(1)} %get-tuple-element.119), channel_id=1, source_target_pairs={{0,8},{8,16},{16,24},{24,0},{1,9},{9,17},{17,25},{25,1},{2,10},{10... | collective-permute-start | bytes 1572872 | tf_op jit(solution)/shard_map/ppermute | solution.py:18
  112.4 25.9 %collective-permute-start.42 = (bf16[64,4096]{1,0:T(8,128)(2,1)S(1)}, bf16[64,4096]{1,0:T(8,128)(2,1)S(1)}, u32[]{:S(2)}, u32[]{:S(2)}) collective-permute-start(bf16[64,4096]{1,0:T(8,128)(2,1)S(1)} %get-tuple-element.126), channel_id=1, source_target_pairs={{0,24},{8,0},{16,8},{24,16},{1,25},{9,1},{17,9},{25,17},{2,26},{10... | collective-permute-start | bytes 1572872 | tf_op jit(solution)/shard_map/ppermute | solution.py:18
  114.2 12.3 %collective-permute-start.28 = (bf16[64,4096]{1,0:T(8,128)(2,1)S(1)}, bf16[64,4096]{1,0:T(8,128)(2,1)S(1)}, u32[]{:S(2)}, u32[]{:S(2)}) collective-permute-start(bf16[64,4096]{1,0:T(8,128)(2,1)S(1)} %get-tuple-element.105), channel_id=1, source_target_pairs={{0,6},{2,0},{4,2},{6,4},{1,7},{3,1},{5,3},{7,5},{8,14},{10,8},{12,... | collective-permute-start | bytes 1572872 | tf_op jit(solution)/shard_map/ppermute | solution.py:18
  123.0 12.2 %collective-permute-start.29 = (bf16[64,4096]{1,0:T(8,128)(2,1)S(1)}, bf16[64,4096]{1,0:T(8,128)(2,1)S(1)}, u32[]{:S(2)}, u32[]{:S(2)}) collective-permute-start(bf16[64,4096]{1,0:T(8,128)(2,1)S(1)} %get-tuple-element.106), channel_id=1, source_target_pairs={{0,2},{2,4},{4,6},{6,0},{1,3},{3,5},{5,7},{7,1},{8,10},{10,12},{12... | collective-permute-start | bytes 1572872 | tf_op jit(solution)/shard_map/ppermute | solution.py:18
  123.3 15.2 %collective-permute-start.31 = (bf16[64,4096]{1,0:T(8,128)(2,1)S(1)}, bf16[64,4096]{1,0:T(8,128)(2,1)S(1)}, u32[]{:S(2)}, u32[]{:S(2)}) collective-permute-start(bf16[64,4096]{1,0:T(8,128)(2,1)S(1)} %get-tuple-element.115), channel_id=1, source_target_pairs={{0,6},{2,0},{4,2},{6,4},{1,7},{3,1},{5,3},{7,5},{8,14},{10,8},{12,... | collective-permute-start | bytes 1572872 | tf_op jit(solution)/shard_map/ppermute | solution.py:18
  126.5 15.8 %collective-permute-start.27 = (bf16[64,4096]{1,0:T(8,128)(2,1)S(1)}, bf16[64,4096]{1,0:T(8,128)(2,1)S(1)}, u32[]{:S(2)}, u32[]{:S(2)}) collective-permute-start(bf16[64,4096]{1,0:T(8,128)(2,1)S(1)} %get-tuple-element.96), channel_id=1, source_target_pairs={{0,2},{2,4},{4,6},{6,0},{1,3},{3,5},{5,7},{7,1},{8,10},{10,12},{12... | collective-permute-start | bytes 1572872 | tf_op jit(solution)/shard_map/ppermute | solution.py:18
  135.2 10.8 %collective-permute-start.41 = (bf16[64,4096]{1,0:T(8,128)(2,1)S(1)}, bf16[64,4096]{1,0:T(8,128)(2,1)S(1)}, u32[]{:S(2)}, u32[]{:S(2)}) collective-permute-start(bf16[64,4096]{1,0:T(8,128)(2,1)S(1)} %add_convert_fusion.3), channel_id=1, source_target_pairs={{0,24},{8,0},{16,8},{24,16},{1,25},{9,1},{17,9},{25,17},{2,26},{10... | collective-permute-start | bytes 1572872 | tf_op jit(solution)/shard_map/ppermute | solution.py:18
  138.3 11.7 %collective-permute-start.43 = (bf16[64,4096]{1,0:T(8,128)(2,1)S(1)}, bf16[64,4096]{1,0:T(8,128)(2,1)S(1)}, u32[]{:S(2)}, u32[]{:S(2)}) collective-permute-start(bf16[64,4096]{1,0:T(8,128)(2,1)S(1)} %add_convert_fusion.1), channel_id=1, source_target_pairs={{0,8},{8,16},{16,24},{24,0},{1,9},{9,17},{17,25},{25,1},{2,10},{10... | collective-permute-start | bytes 1572872 | tf_op jit(solution)/shard_map/ppermute | solution.py:18
  138.4 13.3 %collective-permute-start.32 = (bf16[64,4096]{1,0:T(8,128)(2,1)S(1)}, bf16[64,4096]{1,0:T(8,128)(2,1)S(1)}, u32[]{:S(2)}, u32[]{:S(2)}) collective-permute-start(bf16[64,4096]{1,0:T(8,128)(2,1)S(1)} %add_convert_fusion.5), channel_id=1, source_target_pairs={{0,2},{2,4},{4,6},{6,0},{1,3},{3,5},{5,7},{7,1},{8,10},{10,12},{12... | collective-permute-start | bytes 1572872 | tf_op jit(solution)/shard_map/ppermute | solution.py:18
  138.5 13.2 %collective-permute-start.30 = (bf16[64,4096]{1,0:T(8,128)(2,1)S(1)}, bf16[64,4096]{1,0:T(8,128)(2,1)S(1)}, u32[]{:S(2)}, u32[]{:S(2)}) collective-permute-start(bf16[64,4096]{1,0:T(8,128)(2,1)S(1)} %add_convert_fusion.7), channel_id=1, source_target_pairs={{0,6},{2,0},{4,2},{6,4},{1,7},{3,1},{5,3},{7,5},{8,14},{10,8},{12,... | collective-permute-start | bytes 1572872 | tf_op jit(solution)/shard_map/ppermute | solution.py:18
  (20 other events, 142.9 us)
where the time goes:
time: 183 us; the launch traced here: 182 us
  starting transfers between devices  73.5 us (40%)
  waiting for transfers between devices  61.2 us (33%)
  Pallas kernels  37.7 us (21%)
  other arithmetic  5.54 us (3%)
  matrix products  2.35 us (1%)
    ppermute x46, starting transfers between devices, shift(): return lax.ppermute(v, axis, [(i, (i + step) % RING) for i in range(RING)])  72.7 us
    ppermute x46, waiting for transfers between devices, shift(): return lax.ppermute(v, axis, [(i, (i + step) % RING) for i in range(RING)])  58.9 us
    pallas_call x4, Pallas kernels, ffn(): pl.pallas_call(functools.partial(ffn_kernel, rows, looped), out_shape=[pl...  29.1 us
    pallas_call x1, Pallas kernels, load(): pl.pallas_call(load_kernel, out_shape=[pltpu.VMEM((2 * CORES * part, widt...  4.38 us
    pallas_call x1, Pallas kernels, pick(): pl.pallas_call(pick_kernel, out_shape=[pltpu.VMEM(w.shape[1:], BF16) for...  4.23 us
  transfers between devices with their start and end apart: 51, of which 20 were waited for; matrix products, arithmetic and copies ran while one was open for 1% of the time, Pallas kernels for 17%

commit v1 on v0

--- a/solution.py
+++ b/solution.py
@@ -14,8 +14,21 @@
 BF16 = jnp.bfloat16
 
 
-def shift(v, axis, step):
-    return lax.ppermute(v, axis, [(i, (i + step) % RING) for i in range(RING)])
+def shift(v, step):
+    return lax.ppermute(v, "task", [(i, (i + step) % RING) for i in range(RING)])
+
+
+def hop(v, phase, step):
+    pairs = []
+    for x in range(RING):
+        for z in range(RING):
+            for core in range(CORES):
+                on_x = (core == 0) == (phase == 1)
+                to_x = (x + step * on_x) % RING
+                to_z = (z + step * (not on_x)) % RING
+                source = (x * RING + z) * CORES + core
+                pairs.append((source, (to_x * RING + to_z) * CORES + core))
+    return lax.ppermute(v, ("x", "z", "core"), pairs)
 
 
 def swap_cores(v):
@@ -155,10 +168,10 @@
     )(*[in_vmem(v) for v in xs], in_vmem(w1), in_vmem(w2))
 
 
-def ring_gather(v, axis):
+def ring_gather(v, phase):
     half = v.shape[0] // 2
-    plus, minus = shift(v, axis, 1), shift(v, axis, -1)
-    plus2, minus2 = shift(plus[:half], axis, 1), shift(minus[half:], axis, -1)
+    plus, minus = hop(v, phase, 1), hop(v, phase, -1)
+    plus2, minus2 = hop(plus[:half], phase, 1), hop(minus[half:], phase, -1)
     return jnp.concatenate([v, plus, minus, plus2, minus2], axis=0)
 
 
@@ -169,33 +182,33 @@
     return total.astype(BF16)
 
 
-def ring_scatter(v, axis):
+def ring_scatter(v, phase):
     unit = v.shape[0] // RING
     half = unit // 2
     own, plus, minus = v[:unit], v[unit : 2 * unit], v[2 * unit : 3 * unit]
     plus2, minus2 = v[3 * unit : 3 * unit + half], v[3 * unit + half :]
-    from_next, from_last = shift(plus2, axis, -1), shift(minus2, axis, 1)
+    from_next, from_last = hop(plus2, phase, -1), hop(minus2, phase, 1)
     plus = jnp.concatenate([add(plus[:half], from_next), plus[half:]], axis=0)
     minus = jnp.concatenate([minus[:half], add(minus[half:], from_last)], axis=0)
-    return add(own, shift(plus, axis, -1), shift(minus, axis, 1))
-
-
-def first_halves(v, axis):
+    return add(own, hop(plus, phase, -1), hop(minus, phase, 1))
+
+
+def first_halves(v, phase):
     half = v.shape[0] // 2
-    return [shift(v[:half], axis, 1), shift(v[half:], axis, -1)]
-
-
-def second_halves(v, axis):
+    return [hop(v[:half], phase, 1), hop(v[half:], phase, -1)]
+
+
+def second_halves(v, phase):
     half = v.shape[0] // 2
-    return [shift(v[half:], axis, 1), shift(v[:half], axis, -1)]
-
-
-def onward(pair, axis):
-    return [shift(pair[0], axis, 1), shift(pair[1], axis, -1)]
-
-
-def backward(pair, axis):
-    return [shift(pair[0], axis, -1), shift(pair[1], axis, 1)]
+    return [hop(v[half:], phase, 1), hop(v[:half], phase, -1)]
+
+
+def onward(pair, phase):
+    return [hop(pair[0], phase, 1), hop(pair[1], phase, -1)]
+
+
+def backward(pair, phase):
+    return [hop(pair[0], phase, -1), hop(pair[1], phase, 1)]
 
 
 def after(*lists):
@@ -248,36 +261,30 @@
         at = slice(k * CAP, (k + 1) * CAP)
         return jnp.concatenate([kept[at], swapped[at]], axis=0)
 
-    groups = [for_group(0)] + [shift(for_group(k), "task", k) for k in range(1, RING)]
-    a0 = ring_gather(jnp.concatenate(groups[:2], axis=0), "x")
-    b0 = ring_gather(jnp.concatenate(groups[2:], axis=0), "z")
-    lead_a, lead_b = first_halves(a0, "z"), first_halves(b0, "x")
-    rest_a, rest_b = second_halves(a0, "z"), second_halves(b0, "x")
-    (a0, b0), peers = after([a0, b0], peers)
+    groups = [for_group(0)] + [shift(for_group(k), k) for k in range(1, RING)]
+    rows = ring_gather(jnp.concatenate(groups, axis=0), 1)
+    lead = first_halves(rows, 2)
+    rest = second_halves(rows, 2)
+    (rows,), peers = after([rows], peers)
     w1, w2 = load(core_arg, w_gate, peers[0], w_up, peers[1], w_down, peers[2])
-    (w1, w2), lead_a, lead_b = after([w1, w2], lead_a, lead_b)
-    far_a, far_b = onward(lead_a, "z"), onward(lead_b, "x")
-    y0 = ffn([a0, b0], w1, w2, looped=True)
-    y0, rest_a, rest_b = after(y0, rest_a, rest_b)
-    early = ffn(rest_a + rest_b, w1, w2)
-    early, far_a, far_b = after(early, far_a, far_b)
-    early_a, early_b = backward(early[:2], "z"), backward(early[2:], "x")
-    far = ffn(far_a + far_b, w1, w2)
-    far, lead_a, lead_b = after(far, lead_a, lead_b)
-    far_a, far_b = backward(far[:2], "z"), backward(far[2:], "x")
-    late = ffn(lead_a + lead_b, w1, w2)
-    far_a, late_a = after(far_a, late[:2])
-    far_b, late_b = after(far_b, late[2:])
-    late_a = backward([add(v, w) for v, w in zip(late_a, far_a)], "z")
-    late_b = backward([add(v, w) for v, w in zip(late_b, far_b)], "x")
-    ya = collect(y0[0], early_a, late_a)
-    yb = collect(y0[1], early_b, late_b)
-    done_a = ring_scatter(ya, "x")
-    done_b = ring_scatter(yb, "z")
-
-    both = 2 * CAP
-    groups = [done_a[:both], done_a[both:], done_b[:both], done_b[both:]]
-    groups = [groups[0]] + [shift(groups[k], "task", -k) for k in range(1, RING)]
+    (w1, w2), lead = after([w1, w2], lead)
+    far = onward(lead, 2)
+    own = ffn([rows], w1, w2)
+    own, rest = after(own, rest)
+    early = ffn(rest, w1, w2)
+    early, far = after(early, far)
+    early = backward(early, 2)
+    far = ffn(far, w1, w2)
+    far, lead = after(far, lead)
+    far = backward(far, 2)
+    late = ffn(lead, w1, w2)
+    far, late = after(far, late)
+    late = backward([add(v, w) for v, w in zip(late, far)], 2)
+    done = ring_scatter(collect(own[0], early, late), 1)
+
+    both = CORES * CAP
+    groups = [done[k * both : (k + 1) * both] for k in range(RING)]
+    groups = [groups[0]] + [shift(groups[k], -k) for k in range(1, RING)]
     kept = jnp.concatenate([v[:CAP] for v in groups], axis=0)
     swapped = swap_cores(jnp.concatenate([v[CAP:] for v in groups], axis=0))
     wanted = jnp.take(slot_index, order)

time: 183 us -> 159 us (0.87)
  starting transfers between devices: 73.5 us -> 46 us
  waiting for transfers between devices: 61.2 us -> 66.4 us
    ppermute x46 -> x26, starting transfers between devices: 72.7 us -> 45.2 us  [the longest x20 33.3 us: hop(): return lax.ppermute(v, ('x', 'z', 'core'), pairs)]
    ppermute x46 -> x26, waiting for transfers between devices: 58.9 us -> 64.1 us  [the longest x20 59.5 us: hop(): return lax.ppermute(v, ('x', 'z', 'core'), pairs)]
  transfers between devices with their start and end apart: 51 -> 31, of which waited for: 20 -> 16; matrix products, arithmetic and copies ran while one was open for 1% -> 1% of each run, Pallas kernels for 17% -> 18%
where the time goes in v1:
time: 159 us; the launch traced here: 158 us
  waiting for transfers between devices  66.4 us (42%)
  starting transfers between devices  46 us (29%)
  Pallas kernels  36.2 us (23%)
  other arithmetic  5.52 us (3%)
  matrix products  2.35 us (1%)
    ppermute x20, waiting for transfers between devices, hop(): return lax.ppermute(v, ('x', 'z', 'core'), pairs)  59.5 us
    ppermute x20, starting transfers between devices, hop(): return lax.ppermute(v, ('x', 'z', 'core'), pairs)  33.3 us
    pallas_call x4, Pallas kernels, ffn(): pl.pallas_call(functools.partial(ffn_kernel, rows, looped), out_shape=[pl...  27.5 us
    ppermute x6, starting transfers between devices, shift(): lax.ppermute(v, 'task', [(i, (i + step) % RING) for i in range(RING)])  11.9 us
    ppermute x6, waiting for transfers between devices, shift(): lax.ppermute(v, 'task', [(i, (i + step) % RING) for i in range(RING)])  4.62 us
    pallas_call x1, Pallas kernels, load(): pl.pallas_call(load_kernel, out_shape=[pltpu.VMEM((2 * CORES * part, widt...  4.38 us
    pallas_call x1, Pallas kernels, pick(): pl.pallas_call(pick_kernel, out_shape=[pltpu.VMEM(w.shape[1:], BF16) for...  4.23 us
  transfers between devices with their start and end apart: 31, of which 16 were waited for; matrix products, arithmetic and copies ran while one was open for 1% of the time, Pallas kernels for 18%

profile of v1, /device:TPU:0, one launch (start us, length us, event | category | flops | bytes accessed | tf_op | source)
XLA Modules:
  0.0 158.2 jit_solution(14169710021060233500)
XLA Ops:
  6.5 1.8 %collective-permute-start.1 = (bf16[16,4096]{1,0:T(8,128)(2,1)S(1)}, bf16[16,4096]{1,0:T(8,128)(2,1)S(1)}, u32[]{:S(2)}, u32[]{:S(2)}) collective-permute-start(bf16[16,4096]{1,0:T(8,128)(2,1)S(1)} %pad_maximum_fusion.3), channel_id=1, source_target_pairs={{0,32},{32,64},{64,96},{96,0},{1,33},{33,65},{65,97},{97,1},{2,34}... | collective-permute-start | bytes 393224 | tf_op jit(solution)/shard_map/ppermute | solution.py:18
  8.3 3.0 %collective-permute-start.2 = (bf16[16,4096]{1,0:T(8,128)(2,1)S(1)}, bf16[16,4096]{1,0:T(8,128)(2,1)S(1)}, u32[]{:S(2)}, u32[]{:S(2)}) collective-permute-start(bf16[16,4096]{1,0:T(8,128)(2,1)S(1)} %pad_maximum_fusion.4), channel_id=1, source_target_pairs={{0,64},{32,96},{64,0},{96,32},{1,65},{33,97},{65,1},{97,33},{2,66}... | collective-permute-start | bytes 393224 | tf_op jit(solution)/shard_map/ppermute | solution.py:18
  12.7 4.2 %pick.1 = (bf16[448,4096]{1,0:T(8,128)(2,1)S(1)}, bf16[448,4096]{1,0:T(8,128)(2,1)S(1)}, bf16[448,4096]{1,0:T(8,128)(2,1)S(1)}) custom-call(s32[1]{0:T(128)S(6)} %sub.23.which_ref, bf16[2,448,4096]{2,1,0:T(8,128)(2,1)} %bitcast.4, bf16[2,448,4096]{2,1,0:T(8,128)(2,1)} %bitcast.6, bf16[2,448,4096]{2,1,0:T(8,128)(2,1)} %wd.3), custom_call_target="tpu_custom_call" | custom-call | tf_op jit(solution)/shard_map/pick/pallas_call | solution.py:70
  21.0 7.2 %collective-permute-done.4 = bf16[64,4096]{1,0:T(8,128)(2,1)S(1)} collective-permute-done((bf16[64,4096]{1,0:T(8,128)(2,1)S(1)}, bf16[64,4096]{1,0:T(8,128)(2,1)S(1)}, u32[]{:S(2)}, u32[]{:S(2)}) %collective-permute-start.4) | collective-permute-done | bytes 524320 | tf_op jit(solution)/shard_map/ppermute | solution.py:31
  28.6 3.0 %collective-permute-start.7 = (bf16[32,4096]{1,0:T(8,128)(2,1)S(1)}, bf16[32,4096]{1,0:T(8,128)(2,1)S(1)}, u32[]{:S(2)}, u32[]{:S(2)}) collective-permute-start(bf16[32,4096]{1,0:T(8,128)(2,1)S(1)} %slice.152), channel_id=1, source_target_pairs={{0,24},{1,7},{2,26},{3,1},{4,28},{5,3},{6,30},{7,5},{8,0},{9,15},{... | collective-permute-start | bytes 786440 | tf_op jit(solution)/shard_map/ppermute | solution.py:31
  31.8 4.0 %collective-permute-done.6 = bf16[32,4096]{1,0:T(8,128)(2,1)S(1)} collective-permute-done((bf16[32,4096]{1,0:T(8,128)(2,1)S(1)}, bf16[32,4096]{1,0:T(8,128)(2,1)S(1)}, u32[]{:S(2)}, u32[]{:S(2)}) %collective-permute-start.6) | collective-permute-done | bytes 262176 | tf_op jit(solution)/shard_map/ppermute | solution.py:31
  35.9 1.9 %collective-permute-start.11 = (bf16[128,4096]{1,0:T(8,128)(2,1)S(1)}, bf16[128,4096]{1,0:T(8,128)(2,1)S(1)}, u32[]{:S(2)}, u32[]{:S(2)}) collective-permute-start(bf16[128,4096]{1,0:T(8,128)(2,1)S(1)} %get-tuple-element.89), channel_id=1, source_target_pairs={{0,2},{1,9},{2,4},{3,11},{4,6},{5,13},{6,0},{7,15},{8,10},{9,17},{... | collective-permute-start | bytes 3145736 | tf_op jit(solution)/shard_map/ppermute | solution.py:31
  37.9 2.3 %collective-permute-start.12 = (bf16[128,4096]{1,0:T(8,128)(2,1)S(1)}, bf16[128,4096]{1,0:T(8,128)(2,1)S(1)}, u32[]{:S(2)}, u32[]{:S(2)}) collective-permute-start(bf16[128,4096]{1,0:T(8,128)(2,1)S(1)} %get-tuple-element.97), channel_id=1, source_target_pairs={{0,6},{1,25},{2,0},{3,27},{4,2},{5,29},{6,4},{7,31},{8,14},{9,1},{... | collective-permute-start | bytes 3145736 | tf_op jit(solution)/shard_map/ppermute | solution.py:31
  40.2 2.0 %collective-permute-start.14 = (bf16[128,4096]{1,0:T(8,128)(2,1)S(1)}, bf16[128,4096]{1,0:T(8,128)(2,1)S(1)}, u32[]{:S(2)}, u32[]{:S(2)}) collective-permute-start(bf16[128,4096]{1,0:T(8,128)(2,1)S(1)} %get-tuple-element.89), channel_id=1, source_target_pairs={{0,6},{1,25},{2,0},{3,27},{4,2},{5,29},{6,4},{7,31},{8,14},{9,1},{... | collective-permute-start | bytes 3145736 | tf_op jit(solution)/shard_map/ppermute | solution.py:31
  42.2 4.4 %load.1 = (bf16[1792,4096]{1,0:T(8,128)(2,1)S(1)}, bf16[896,4096]{1,0:T(8,128)(2,1)S(1)}) custom-call(s32[1]{0:T(128)} %bitcast.core_ref, bf16[2,448,4096]{2,1,0:T(8,128)(2,1)} %bitcast.5, bf16[448,4096]{1,0:T(8,128)(2,1)S(1)} %collective-permute-done.8.wpg, bf16[2,448,4096]{2,1,0:T(8,128)(2,1)} %bitcast.7, ...), custom_call_target="tpu_custom_call" | custom-call | tf_op jit(solution)/shard_map/load/pallas_call | solution.py:98
  46.6 6.2 %collective-permute-done.11.refs_0_ = bf16[128,4096]{1,0:T(8,128)(2,1)S(1)} collective-permute-done((bf16[128,4096]{1,0:T(8,128)(2,1)S(1)}, bf16[128,4096]{1,0:T(8,128)(2,1)S(1)}, u32[]{:S(2)}, u32[]{:S(2)}) %collective-permute-start.11) | collective-permute-done | bytes 1048608 | tf_op jit(solution)/shard_map/ppermute | solution.py:31
  52.8 2.0 %collective-permute-start.15 = (bf16[128,4096]{1,0:T(8,128)(2,1)S(1)}, bf16[128,4096]{1,0:T(8,128)(2,1)S(1)}, u32[]{:S(2)}, u32[]{:S(2)}) collective-permute-start(bf16[128,4096]{1,0:T(8,128)(2,1)S(1)} %collective-permute-done.11.refs_0_), channel_id=1, source_target_pairs={{0,2},{1,9},{2,4},{3,11},{4,6},{5,13},{6,0},{7,15},{8,10},{9,17},{... | collective-permute-start | bytes 3145736 | tf_op jit(solution)/shard_map/ppermute | solution.py:31
  56.2 6.9 %ffn.4 = bf16[256,4096]{1,0:T(8,128)(2,1)S(1)} custom-call(bf16[256,4096]{1,0:T(8,128)(2,1)S(1)} %get-tuple-element.46.refs_0_, bf16[1792,4096]{1,0:T(8,128)(2,1)S(1)} %get-tuple-element.52.refs_1_.refs_2_, bf16[896,4096]{1,0:T(8,128)(2,1)S(1)} %get-tuple-element.53.refs_2_.refs_3_), custom_call_target="tpu_custom_call" | custom-call | flops 5637144576 | tf_op jit(solution)/shard_map/ffn/pallas_call | solution.py:153
  64.0 6.9 %ffn.5 = (bf16[128,4096]{1,0:T(8,128)(2,1)S(1)}, bf16[128,4096]{1,0:T(8,128)(2,1)S(1)}) custom-call(bf16[128,4096]{1,0:T(8,128)(2,1)S(1)} %collective-permute-done.13.refs_0_, bf16[128,4096]{1,0:T(8,128)(2,1)S(1)} %collective-permute-done.14.refs_1_, bf16[1792,4096]{1,0:T(8,128)(2,1)S(1)} %get-tuple-element.52.refs_1_.refs_2_, ...), custom_call_target="tpu_custom_call" | custom-call | flops 5637144576 | tf_op jit(solution)/shard_map/ffn/pallas_call | solution.py:153
  70.9 4.4 %collective-permute-done.15.refs_0_ = bf16[128,4096]{1,0:T(8,128)(2,1)S(1)} collective-permute-done((bf16[128,4096]{1,0:T(8,128)(2,1)S(1)}, bf16[128,4096]{1,0:T(8,128)(2,1)S(1)}, u32[]{:S(2)}, u32[]{:S(2)}) %collective-permute-start.15) | collective-permute-done | bytes 1048608 | tf_op jit(solution)/shard_map/ppermute | solution.py:31
  75.2 6.9 %ffn.6 = (bf16[128,4096]{1,0:T(8,128)(2,1)S(1)}, bf16[128,4096]{1,0:T(8,128)(2,1)S(1)}) custom-call(bf16[128,4096]{1,0:T(8,128)(2,1)S(1)} %collective-permute-done.15.refs_0_, bf16[128,4096]{1,0:T(8,128)(2,1)S(1)} %collective-permute-done.16.refs_1_, bf16[1792,4096]{1,0:T(8,128)(2,1)S(1)} %get-tuple-element.52.refs_1_.refs_2_, ...), custom_call_target="tpu_custom_call" | custom-call | flops 5637144576 | tf_op jit(solution)/shard_map/ffn/pallas_call | solution.py:153
  82.2 3.5 %collective-permute-start.18 = (bf16[128,4096]{1,0:T(8,128)(2,1)S(1)}, bf16[128,4096]{1,0:T(8,128)(2,1)S(1)}, u32[]{:S(2)}, u32[]{:S(2)}) collective-permute-start(bf16[128,4096]{1,0:T(8,128)(2,1)S(1)} %get-tuple-element.66), channel_id=1, source_target_pairs={{0,6},{1,25},{2,0},{3,27},{4,2},{5,29},{6,4},{7,31},{8,14},{9,1},{... | collective-permute-start | bytes 3145736 | tf_op jit(solution)/shard_map/ppermute | solution.py:31
  86.2 2.6 %collective-permute-start.21 = (bf16[128,4096]{1,0:T(8,128)(2,1)S(1)}, bf16[128,4096]{1,0:T(8,128)(2,1)S(1)}, u32[]{:S(2)}, u32[]{:S(2)}) collective-permute-start(bf16[128,4096]{1,0:T(8,128)(2,1)S(1)} %get-tuple-element.74), channel_id=1, source_target_pairs={{0,6},{1,25},{2,0},{3,27},{4,2},{5,29},{6,4},{7,31},{8,14},{9,1},{... | collective-permute-start | bytes 3145736 | tf_op jit(solution)/shard_map/ppermute | solution.py:31
  88.9 6.9 %ffn.7 = (bf16[128,4096]{1,0:T(8,128)(2,1)S(1)}, bf16[128,4096]{1,0:T(8,128)(2,1)S(1)}) custom-call(bf16[128,4096]{1,0:T(8,128)(2,1)S(1)} %collective-permute-done.11.refs_0_, bf16[128,4096]{1,0:T(8,128)(2,1)S(1)} %collective-permute-done.12.refs_1_, bf16[1792,4096]{1,0:T(8,128)(2,1)S(1)} %get-tuple-element.52.refs_1_.refs_2_, ...), custom_call_target="tpu_custom_call" | custom-call | flops 5637144576 | tf_op jit(solution)/shard_map/ffn/pallas_call | solution.py:153
  95.8 2.2 %collective-permute-done.18 = bf16[128,4096]{1,0:T(8,128)(2,1)S(1)} collective-permute-done((bf16[128,4096]{1,0:T(8,128)(2,1)S(1)}, bf16[128,4096]{1,0:T(8,128)(2,1)S(1)}, u32[]{:S(2)}, u32[]{:S(2)}) %collective-permute-start.18) | collective-permute-done | bytes 1048608 | tf_op jit(solution)/shard_map/ppermute | solution.py:31
  97.9 3.7 %collective-permute-done.19 = bf16[128,4096]{1,0:T(8,128)(2,1)S(1)} collective-permute-done((bf16[128,4096]{1,0:T(8,128)(2,1)S(1)}, bf16[128,4096]{1,0:T(8,128)(2,1)S(1)}, u32[]{:S(2)}, u32[]{:S(2)}) %collective-permute-start.19) | collective-permute-done | bytes 1048608 | tf_op jit(solution)/shard_map/ppermute | solution.py:31
  102.2 2.1 %collective-permute-start.22 = (bf16[128,4096]{1,0:T(8,128)(2,1)S(1)}, bf16[128,4096]{1,0:T(8,128)(2,1)S(1)}, u32[]{:S(2)}, u32[]{:S(2)}) collective-permute-start(bf16[128,4096]{1,0:T(8,128)(2,1)S(1)} %add_convert_fusion.1), channel_id=1, source_target_pairs={{0,2},{1,9},{2,4},{3,11},{4,6},{5,13},{6,0},{7,15},{8,10},{9,17},{... | collective-permute-start | bytes 3145736 | tf_op jit(solution)/shard_map/ppermute | solution.py:31
  104.3 8.6 %collective-permute-done.17 = bf16[128,4096]{1,0:T(8,128)(2,1)S(1)} collective-permute-done((bf16[128,4096]{1,0:T(8,128)(2,1)S(1)}, bf16[128,4096]{1,0:T(8,128)(2,1)S(1)}, u32[]{:S(2)}, u32[]{:S(2)}) %collective-permute-start.17) | collective-permute-done | bytes 1048608 | tf_op jit(solution)/shard_map/ppermute | solution.py:31
  112.9 7.5 %collective-permute-done.20 = bf16[128,4096]{1,0:T(8,128)(2,1)S(1)} collective-permute-done((bf16[128,4096]{1,0:T(8,128)(2,1)S(1)}, bf16[128,4096]{1,0:T(8,128)(2,1)S(1)}, u32[]{:S(2)}, u32[]{:S(2)}) %collective-permute-start.20) | collective-permute-done | bytes 1048608 | tf_op jit(solution)/shard_map/ppermute | solution.py:31
  120.4 3.7 %collective-permute-done.22 = bf16[128,4096]{1,0:T(8,128)(2,1)S(1)} collective-permute-done((bf16[128,4096]{1,0:T(8,128)(2,1)S(1)}, bf16[128,4096]{1,0:T(8,128)(2,1)S(1)}, u32[]{:S(2)}, u32[]{:S(2)}) %collective-permute-start.22) | collective-permute-done | bytes 1048608 | tf_op jit(solution)/shard_map/ppermute | solution.py:31
  125.9 4.1 %collective-permute-start.23 = (bf16[32,4096]{1,0:T(8,128)(2,1)S(1)}, bf16[32,4096]{1,0:T(8,128)(2,1)S(1)}, u32[]{:S(2)}, u32[]{:S(2)}) collective-permute-start(bf16[32,4096]{1,0:T(8,128)(2,1)S(1)} %get-tuple-element.79), channel_id=1, source_target_pairs={{0,24},{1,7},{2,26},{3,1},{4,28},{5,3},{6,30},{7,5},{8,0},{9,15},{... | collective-permute-start | bytes 786440 | tf_op jit(solution)/shard_map/ppermute | solution.py:31
  130.0 4.2 %collective-permute-done.25 = bf16[32,4096]{1,0:T(8,128)(2,1)S(1)} collective-permute-done((bf16[32,4096]{1,0:T(8,128)(2,1)S(1)}, bf16[32,4096]{1,0:T(8,128)(2,1)S(1)}, u32[]{:S(2)}, u32[]{:S(2)}) %collective-permute-start.25) | collective-permute-done | bytes 262176 | tf_op jit(solution)/shard_map/ppermute | solution.py:31
  134.6 3.3 %collective-permute-start.24 = (bf16[64,4096]{1,0:T(8,128)(2,1)S(1)}, bf16[64,4096]{1,0:T(8,128)(2,1)S(1)}, u32[]{:S(2)}, u32[]{:S(2)}) collective-permute-start(bf16[64,4096]{1,0:T(8,128)(2,1)S(1)} %pad_maximum_fusion), channel_id=1, source_target_pairs={{0,24},{1,7},{2,26},{3,1},{4,28},{5,3},{6,30},{7,5},{8,0},{9,15},{... | collective-permute-start | bytes 1572872 | tf_op jit(solution)/shard_map/ppermute | solution.py:31
  137.9 7.0 %collective-permute-done.26 = bf16[64,4096]{1,0:T(8,128)(2,1)S(1)} collective-permute-done((bf16[64,4096]{1,0:T(8,128)(2,1)S(1)}, bf16[64,4096]{1,0:T(8,128)(2,1)S(1)}, u32[]{:S(2)}, u32[]{:S(2)}) %collective-permute-start.26) | collective-permute-done | bytes 524320 | tf_op jit(solution)/shard_map/ppermute | solution.py:31
  145.1 2.8 %collective-permute-start.27 = (bf16[16,4096]{1,0:T(8,128)(2,1)S(1)}, bf16[16,4096]{1,0:T(8,128)(2,1)S(1)}, u32[]{:S(2)}, u32[]{:S(2)}) collective-permute-start(bf16[16,4096]{1,0:T(8,128)(2,1)S(1)} %get-tuple-element.86), channel_id=1, source_target_pairs={{0,96},{32,0},{64,32},{96,64},{1,97},{33,1},{65,33},{97,65},{2,98}... | collective-permute-start | bytes 393224 | tf_op jit(solution)/shard_map/ppermute | solution.py:18
  148.0 2.9 %collective-permute-start.28 = (bf16[16,4096]{1,0:T(8,128)(2,1)S(1)}, bf16[16,4096]{1,0:T(8,128)(2,1)S(1)}, u32[]{:S(2)}, u32[]{:S(2)}) collective-permute-start(bf16[16,4096]{1,0:T(8,128)(2,1)S(1)} %get-tuple-element.85), channel_id=1, source_target_pairs={{0,64},{32,96},{64,0},{96,32},{1,65},{33,97},{65,1},{97,33},{2,66}... | collective-permute-start | bytes 393224 | tf_op jit(solution)/shard_map/ppermute | solution.py:18
  150.9 4.4 %collective-permute-done.28 = bf16[16,4096]{1,0:T(8,128)(2,1)S(1)} collective-permute-done((bf16[16,4096]{1,0:T(8,128)(2,1)S(1)}, bf16[16,4096]{1,0:T(8,128)(2,1)S(1)}, u32[]{:S(2)}, u32[]{:S(2)}) %collective-permute-start.28) | collective-permute-done | bytes 131104 | tf_op jit(solution)/shard_map/ppermute | solution.py:18
  (82 shorter events, 21.4 us)
Async XLA Ops:
  4.8 1.6 %collective-permute-start = (bf16[32,4096]{1,0:T(8,128)(2,1)S(1)}, bf16[32,4096]{1,0:T(8,128)(2,1)S(1)}, u32[]{:S(2)}, u32[]{:S(2)}) collective-permute-start(bf16[32,4096]{1,0:T(8,128)(2,1)S(1)} %slice.147), channel_id=1, source_target_pairs={{0,1},{1,0},{2,3},{3,2},{4,5},{5,4},{6,7},{7,6},{8,9},{9,8},{10,11... | collective-permute-start | bytes 786440 | tf_op jit(solution)/shard_map/ppermute | solution.py:35
  6.5 11.0 %collective-permute-start.1 = (bf16[16,4096]{1,0:T(8,128)(2,1)S(1)}, bf16[16,4096]{1,0:T(8,128)(2,1)S(1)}, u32[]{:S(2)}, u32[]{:S(2)}) collective-permute-start(bf16[16,4096]{1,0:T(8,128)(2,1)S(1)} %pad_maximum_fusion.3), channel_id=1, source_target_pairs={{0,32},{32,64},{64,96},{96,0},{1,33},{33,65},{65,97},{97,1},{2,34}... | collective-permute-start | bytes 393224 | tf_op jit(solution)/shard_map/ppermute | solution.py:18
  8.3 9.4 %collective-permute-start.2 = (bf16[16,4096]{1,0:T(8,128)(2,1)S(1)}, bf16[16,4096]{1,0:T(8,128)(2,1)S(1)}, u32[]{:S(2)}, u32[]{:S(2)}) collective-permute-start(bf16[16,4096]{1,0:T(8,128)(2,1)S(1)} %pad_maximum_fusion.4), channel_id=1, source_target_pairs={{0,64},{32,96},{64,0},{96,32},{1,65},{33,97},{65,1},{97,33},{2,66}... | collective-permute-start | bytes 393224 | tf_op jit(solution)/shard_map/ppermute | solution.py:18
  11.3 6.4 %collective-permute-start.3 = (bf16[16,4096]{1,0:T(8,128)(2,1)S(1)}, bf16[16,4096]{1,0:T(8,128)(2,1)S(1)}, u32[]{:S(2)}, u32[]{:S(2)}) collective-permute-start(bf16[16,4096]{1,0:T(8,128)(2,1)S(1)} %pad_maximum_fusion.5), channel_id=1, source_target_pairs={{0,96},{32,0},{64,32},{96,64},{1,97},{33,1},{65,33},{97,65},{2,98}... | collective-permute-start | bytes 393224 | tf_op jit(solution)/shard_map/ppermute | solution.py:18
  16.9 23.3 %collective-permute-start.8 = (bf16[448,4096]{1,0:T(8,128)(2,1)S(1)}, bf16[448,4096]{1,0:T(8,128)(2,1)S(1)}, u32[]{:S(2)}, u32[]{:S(2)}) collective-permute-start(bf16[448,4096]{1,0:T(8,128)(2,1)S(1)} %get-tuple-element.43), channel_id=1, source_target_pairs={{0,1},{1,0},{2,3},{3,2},{4,5},{5,4},{6,7},{7,6},{8,9},{9,8},{10,11... | collective-permute-start | bytes 11010056 | tf_op jit(solution)/shard_map/ppermute | solution.py:35
  17.0 25.2 %collective-permute-start.9 = (bf16[448,4096]{1,0:T(8,128)(2,1)S(1)}, bf16[448,4096]{1,0:T(8,128)(2,1)S(1)}, u32[]{:S(2)}, u32[]{:S(2)}) collective-permute-start(bf16[448,4096]{1,0:T(8,128)(2,1)S(1)} %get-tuple-element.44), channel_id=1, source_target_pairs={{0,1},{1,0},{2,3},{3,2},{4,5},{5,4},{6,7},{7,6},{8,9},{9,8},{10,11... | collective-permute-start | bytes 11010056 | tf_op jit(solution)/shard_map/ppermute | solution.py:35
  17.5 24.7 %collective-permute-start.10 = (bf16[448,4096]{1,0:T(8,128)(2,1)S(1)}, bf16[448,4096]{1,0:T(8,128)(2,1)S(1)}, u32[]{:S(2)}, u32[]{:S(2)}) collective-permute-start(bf16[448,4096]{1,0:T(8,128)(2,1)S(1)} %get-tuple-element.45), channel_id=1, source_target_pairs={{0,1},{1,0},{2,3},{3,2},{4,5},{5,4},{6,7},{7,6},{8,9},{9,8},{10,11... | collective-permute-start | bytes 11010056 | tf_op jit(solution)/shard_map/ppermute | solution.py:35
  17.7 10.5 %collective-permute-start.4 = (bf16[64,4096]{1,0:T(8,128)(2,1)S(1)}, bf16[64,4096]{1,0:T(8,128)(2,1)S(1)}, u32[]{:S(2)}, u32[]{:S(2)}) collective-permute-start(bf16[64,4096]{1,0:T(8,128)(2,1)S(1)} %get-tuple-element.115), channel_id=1, source_target_pairs={{0,8},{1,3},{2,10},{3,5},{4,12},{5,7},{6,14},{7,1},{8,16},{9,11},{... | collective-permute-start | bytes 1572872 | tf_op jit(solution)/shard_map/ppermute | solution.py:31
  19.3 9.3 %collective-permute-start.5 = (bf16[64,4096]{1,0:T(8,128)(2,1)S(1)}, bf16[64,4096]{1,0:T(8,128)(2,1)S(1)}, u32[]{:S(2)}, u32[]{:S(2)}) collective-permute-start(bf16[64,4096]{1,0:T(8,128)(2,1)S(1)} %get-tuple-element.115), channel_id=1, source_target_pairs={{0,24},{1,7},{2,26},{3,1},{4,28},{5,3},{6,30},{7,5},{8,0},{9,15},{... | collective-permute-start | bytes 1572872 | tf_op jit(solution)/shard_map/ppermute | solution.py:31
  28.2 7.7 %collective-permute-start.6 = (bf16[32,4096]{1,0:T(8,128)(2,1)S(1)}, bf16[32,4096]{1,0:T(8,128)(2,1)S(1)}, u32[]{:S(2)}, u32[]{:S(2)}) collective-permute-start(bf16[32,4096]{1,0:T(8,128)(2,1)S(1)} %slice.151), channel_id=1, source_target_pairs={{0,8},{1,3},{2,10},{3,5},{4,12},{5,7},{6,14},{7,1},{8,16},{9,11},{... | collective-permute-start | bytes 786440 | tf_op jit(solution)/shard_map/ppermute | solution.py:31
  28.6 9.2 %collective-permute-start.7 = (bf16[32,4096]{1,0:T(8,128)(2,1)S(1)}, bf16[32,4096]{1,0:T(8,128)(2,1)S(1)}, u32[]{:S(2)}, u32[]{:S(2)}) collective-permute-start(bf16[32,4096]{1,0:T(8,128)(2,1)S(1)} %slice.152), channel_id=1, source_target_pairs={{0,24},{1,7},{2,26},{3,1},{4,28},{5,3},{6,30},{7,5},{8,0},{9,15},{... | collective-permute-start | bytes 786440 | tf_op jit(solution)/shard_map/ppermute | solution.py:31
  35.9 16.9 %collective-permute-start.11 = (bf16[128,4096]{1,0:T(8,128)(2,1)S(1)}, bf16[128,4096]{1,0:T(8,128)(2,1)S(1)}, u32[]{:S(2)}, u32[]{:S(2)}) collective-permute-start(bf16[128,4096]{1,0:T(8,128)(2,1)S(1)} %get-tuple-element.89), channel_id=1, source_target_pairs={{0,2},{1,9},{2,4},{3,11},{4,6},{5,13},{6,0},{7,15},{8,10},{9,17},{... | collective-permute-start | bytes 3145736 | tf_op jit(solution)/shard_map/ppermute | solution.py:31
  37.9 14.9 %collective-permute-start.12 = (bf16[128,4096]{1,0:T(8,128)(2,1)S(1)}, bf16[128,4096]{1,0:T(8,128)(2,1)S(1)}, u32[]{:S(2)}, u32[]{:S(2)}) collective-permute-start(bf16[128,4096]{1,0:T(8,128)(2,1)S(1)} %get-tuple-element.97), channel_id=1, source_target_pairs={{0,6},{1,25},{2,0},{3,27},{4,2},{5,29},{6,4},{7,31},{8,14},{9,1},{... | collective-permute-start | bytes 3145736 | tf_op jit(solution)/shard_map/ppermute | solution.py:31
  40.2 23.8 %collective-permute-start.14 = (bf16[128,4096]{1,0:T(8,128)(2,1)S(1)}, bf16[128,4096]{1,0:T(8,128)(2,1)S(1)}, u32[]{:S(2)}, u32[]{:S(2)}) collective-permute-start(bf16[128,4096]{1,0:T(8,128)(2,1)S(1)} %get-tuple-element.89), channel_id=1, source_target_pairs={{0,6},{1,25},{2,0},{3,27},{4,2},{5,29},{6,4},{7,31},{8,14},{9,1},{... | collective-permute-start | bytes 3145736 | tf_op jit(solution)/shard_map/ppermute | solution.py:31
  42.2 21.8 %collective-permute-start.13 = (bf16[128,4096]{1,0:T(8,128)(2,1)S(1)}, bf16[128,4096]{1,0:T(8,128)(2,1)S(1)}, u32[]{:S(2)}, u32[]{:S(2)}) collective-permute-start(bf16[128,4096]{1,0:T(8,128)(2,1)S(1)} %get-tuple-element.97), channel_id=1, source_target_pairs={{0,2},{1,9},{2,4},{3,11},{4,6},{5,13},{6,0},{7,15},{8,10},{9,17},{... | collective-permute-start | bytes 3145736 | tf_op jit(solution)/shard_map/ppermute | solution.py:31
  52.8 22.5 %collective-permute-start.15 = (bf16[128,4096]{1,0:T(8,128)(2,1)S(1)}, bf16[128,4096]{1,0:T(8,128)(2,1)S(1)}, u32[]{:S(2)}, u32[]{:S(2)}) collective-permute-start(bf16[128,4096]{1,0:T(8,128)(2,1)S(1)} %collective-permute-done.11.refs_0_), channel_id=1, source_target_pairs={{0,2},{1,9},{2,4},{3,11},{4,6},{5,13},{6,0},{7,15},{8,10},{9,17},{... | collective-permute-start | bytes 3145736 | tf_op jit(solution)/shard_map/ppermute | solution.py:31
  54.8 20.5 %collective-permute-start.16 = (bf16[128,4096]{1,0:T(8,128)(2,1)S(1)}, bf16[128,4096]{1,0:T(8,128)(2,1)S(1)}, u32[]{:S(2)}, u32[]{:S(2)}) collective-permute-start(bf16[128,4096]{1,0:T(8,128)(2,1)S(1)} %collective-permute-done.12.refs_1_), channel_id=1, source_target_pairs={{0,6},{1,25},{2,0},{3,27},{4,2},{5,29},{6,4},{7,31},{8,14},{9,1},{... | collective-permute-start | bytes 3145736 | tf_op jit(solution)/shard_map/ppermute | solution.py:31
  82.2 15.8 %collective-permute-start.18 = (bf16[128,4096]{1,0:T(8,128)(2,1)S(1)}, bf16[128,4096]{1,0:T(8,128)(2,1)S(1)}, u32[]{:S(2)}, u32[]{:S(2)}) collective-permute-start(bf16[128,4096]{1,0:T(8,128)(2,1)S(1)} %get-tuple-element.66), channel_id=1, source_target_pairs={{0,6},{1,25},{2,0},{3,27},{4,2},{5,29},{6,4},{7,31},{8,14},{9,1},{... | collective-permute-start | bytes 3145736 | tf_op jit(solution)/shard_map/ppermute | solution.py:31
  85.6 16.0 %collective-permute-start.19 = (bf16[128,4096]{1,0:T(8,128)(2,1)S(1)}, bf16[128,4096]{1,0:T(8,128)(2,1)S(1)}, u32[]{:S(2)}, u32[]{:S(2)}) collective-permute-start(bf16[128,4096]{1,0:T(8,128)(2,1)S(1)} %get-tuple-element.67), channel_id=1, source_target_pairs={{0,2},{1,9},{2,4},{3,11},{4,6},{5,13},{6,0},{7,15},{8,10},{9,17},{... | collective-permute-start | bytes 3145736 | tf_op jit(solution)/shard_map/ppermute | solution.py:31
  85.6 27.2 %collective-permute-start.17 = (bf16[128,4096]{1,0:T(8,128)(2,1)S(1)}, bf16[128,4096]{1,0:T(8,128)(2,1)S(1)}, u32[]{:S(2)}, u32[]{:S(2)}) collective-permute-start(bf16[128,4096]{1,0:T(8,128)(2,1)S(1)} %get-tuple-element.61), channel_id=1, source_target_pairs={{0,2},{1,9},{2,4},{3,11},{4,6},{5,13},{6,0},{7,15},{8,10},{9,17},{... | collective-permute-start | bytes 3145736 | tf_op jit(solution)/shard_map/ppermute | solution.py:31
  86.2 26.6 %collective-permute-start.21 = (bf16[128,4096]{1,0:T(8,128)(2,1)S(1)}, bf16[128,4096]{1,0:T(8,128)(2,1)S(1)}, u32[]{:S(2)}, u32[]{:S(2)}) collective-permute-start(bf16[128,4096]{1,0:T(8,128)(2,1)S(1)} %get-tuple-element.74), channel_id=1, source_target_pairs={{0,6},{1,25},{2,0},{3,27},{4,2},{5,29},{6,4},{7,31},{8,14},{9,1},{... | collective-permute-start | bytes 3145736 | tf_op jit(solution)/shard_map/ppermute | solution.py:31
  101.9 18.5 %collective-permute-start.20 = (bf16[128,4096]{1,0:T(8,128)(2,1)S(1)}, bf16[128,4096]{1,0:T(8,128)(2,1)S(1)}, u32[]{:S(2)}, u32[]{:S(2)}) collective-permute-start(bf16[128,4096]{1,0:T(8,128)(2,1)S(1)} %add_convert_fusion.3), channel_id=1, source_target_pairs={{0,6},{1,25},{2,0},{3,27},{4,2},{5,29},{6,4},{7,31},{8,14},{9,1},{... | collective-permute-start | bytes 3145736 | tf_op jit(solution)/shard_map/ppermute | solution.py:31
  102.2 21.9 %collective-permute-start.22 = (bf16[128,4096]{1,0:T(8,128)(2,1)S(1)}, bf16[128,4096]{1,0:T(8,128)(2,1)S(1)}, u32[]{:S(2)}, u32[]{:S(2)}) collective-permute-start(bf16[128,4096]{1,0:T(8,128)(2,1)S(1)} %add_convert_fusion.1), channel_id=1, source_target_pairs={{0,2},{1,9},{2,4},{3,11},{4,6},{5,13},{6,0},{7,15},{8,10},{9,17},{... | collective-permute-start | bytes 3145736 | tf_op jit(solution)/shard_map/ppermute | solution.py:31
  125.3 9.0 %collective-permute-start.25 = (bf16[32,4096]{1,0:T(8,128)(2,1)S(1)}, bf16[32,4096]{1,0:T(8,128)(2,1)S(1)}, u32[]{:S(2)}, u32[]{:S(2)}) collective-permute-start(bf16[32,4096]{1,0:T(8,128)(2,1)S(1)} %get-tuple-element.80), channel_id=1, source_target_pairs={{0,8},{1,3},{2,10},{3,5},{4,12},{5,7},{6,14},{7,1},{8,16},{9,11},{... | collective-permute-start | bytes 786440 | tf_op jit(solution)/shard_map/ppermute | solution.py:31
  125.9 12.0 %copy-start = (s32[32]{0:T(128)S(1)}, s32[32]{0:T(128)}, u32[]{:S(2)}) copy-start(s32[32]{0:T(128)} %param.10) | copy-start | bytes 388
  125.9 8.6 %collective-permute-start.23 = (bf16[32,4096]{1,0:T(8,128)(2,1)S(1)}, bf16[32,4096]{1,0:T(8,128)(2,1)S(1)}, u32[]{:S(2)}, u32[]{:S(2)}) collective-permute-start(bf16[32,4096]{1,0:T(8,128)(2,1)S(1)} %get-tuple-element.79), channel_id=1, source_target_pairs={{0,24},{1,7},{2,26},{3,1},{4,28},{5,3},{6,30},{7,5},{8,0},{9,15},{... | collective-permute-start | bytes 786440 | tf_op jit(solution)/shard_map/ppermute | solution.py:31
  134.4 10.5 %collective-permute-start.26 = (bf16[64,4096]{1,0:T(8,128)(2,1)S(1)}, bf16[64,4096]{1,0:T(8,128)(2,1)S(1)}, u32[]{:S(2)}, u32[]{:S(2)}) collective-permute-start(bf16[64,4096]{1,0:T(8,128)(2,1)S(1)} %pad_maximum_fusion.1), channel_id=1, source_target_pairs={{0,8},{1,3},{2,10},{3,5},{4,12},{5,7},{6,14},{7,1},{8,16},{9,11},{... | collective-permute-start | bytes 1572872 | tf_op jit(solution)/shard_map/ppermute | solution.py:31
  134.6 10.3 %collective-permute-start.24 = (bf16[64,4096]{1,0:T(8,128)(2,1)S(1)}, bf16[64,4096]{1,0:T(8,128)(2,1)S(1)}, u32[]{:S(2)}, u32[]{:S(2)}) collective-permute-start(bf16[64,4096]{1,0:T(8,128)(2,1)S(1)} %pad_maximum_fusion), channel_id=1, source_target_pairs={{0,24},{1,7},{2,26},{3,1},{4,28},{5,3},{6,30},{7,5},{8,0},{9,15},{... | collective-permute-start | bytes 1572872 | tf_op jit(solution)/shard_map/ppermute | solution.py:31
  145.1 5.8 %collective-permute-start.27 = (bf16[16,4096]{1,0:T(8,128)(2,1)S(1)}, bf16[16,4096]{1,0:T(8,128)(2,1)S(1)}, u32[]{:S(2)}, u32[]{:S(2)}) collective-permute-start(bf16[16,4096]{1,0:T(8,128)(2,1)S(1)} %get-tuple-element.86), channel_id=1, source_target_pairs={{0,96},{32,0},{64,32},{96,64},{1,97},{33,1},{65,33},{97,65},{2,98}... | collective-permute-start | bytes 393224 | tf_op jit(solution)/shard_map/ppermute | solution.py:18
  147.9 7.7 %collective-permute-start.29 = (bf16[16,4096]{1,0:T(8,128)(2,1)S(1)}, bf16[16,4096]{1,0:T(8,128)(2,1)S(1)}, u32[]{:S(2)}, u32[]{:S(2)}) collective-permute-start(bf16[16,4096]{1,0:T(8,128)(2,1)S(1)} %get-tuple-element.84), channel_id=1, source_target_pairs={{0,32},{32,64},{64,96},{96,0},{1,33},{33,65},{65,97},{97,1},{2,34}... | collective-permute-start | bytes 393224 | tf_op jit(solution)/shard_map/ppermute | solution.py:18
  148.0 7.4 %collective-permute-start.28 = (bf16[16,4096]{1,0:T(8,128)(2,1)S(1)}, bf16[16,4096]{1,0:T(8,128)(2,1)S(1)}, u32[]{:S(2)}, u32[]{:S(2)}) collective-permute-start(bf16[16,4096]{1,0:T(8,128)(2,1)S(1)} %get-tuple-element.85), channel_id=1, source_target_pairs={{0,64},{32,96},{64,0},{96,32},{1,65},{33,97},{65,1},{97,33},{2,66}... | collective-permute-start | bytes 393224 | tf_op jit(solution)/shard_map/ppermute | solution.py:18
  155.6 1.6 %collective-permute-start.30 = (bf16[32,4096]{1,0:T(8,128)(2,1)S(1)}, bf16[32,4096]{1,0:T(8,128)(2,1)S(1)}, u32[]{:S(2)}, u32[]{:S(2)}) collective-permute-start(bf16[32,4096]{1,0:T(8,128)(2,1)S(1)} %pad_maximum_fusion.2), channel_id=1, source_target_pairs={{0,1},{1,0},{2,3},{3,2},{4,5},{5,4},{6,7},{7,6},{8,9},{9,8},{10,11... | collective-permute-start | bytes 786440 | tf_op jit(solution)/shard_map/ppermute | solution.py:35
